TPU v7x, 128 devices: a whole 4x4x4 slice. The times are simulated.
128 devices in a mesh: slab: 4 (over x), row: 2 (over core), col: 16 (over z, y).
Axes of the slice: x: 4, y: 4, z: 4, core: 2. Of those that a mesh axis runs over, the one named last changes fastest.
Arguments:
- sources: float32 [4, 16, 2, 384, 256], P('slab', 'col', 'row'), may hold values from -6 to 6
- tr_vals: float32 [4, 16, 2, 6, 12, 128, 128], P('slab', 'col', 'row'), may hold values from -0.09375 to 0.09375
- tr_cols: int32 [4, 16, 2, 6, 12], P('slab', 'col', 'row'), may hold values from 0 to 47, as said below
- rf_vals: float32 [4, 16, 2, 6, 12, 128, 128], P('slab', 'col', 'row'), may hold values from -0.078125 to 0.078125
- rf_cols: int32 [4, 16, 2, 6, 12], P('slab', 'col', 'row'), may hold values from 0 to 47, as said below
Outputs:
- total_traces: float32 [4, 16, 2, 384, 256], P('slab', 'col', 'row')
Inputs may be any that keep to these rules, and one draw needn't show every extreme that they name: `tr_cols`: each block row lists 12 different column blocks of its column group. `rf_cols`: each block row lists 12 different column blocks of its column group.
All inputs are finite; a program needn't handle non-finite values.
Results may differ from a plain program's by a relative error of at most 0.0001.
Values sent between devices are 32-bit elements; how exact they have to be, the bound alone decides.
A program may use at most 128 MiB of HBM per device.

v0:
```python
import jax
import jax.numpy as jnp
from jax import lax
from jax.sharding import PartitionSpec as P


def passed_along(value, axis, steps):
    count = lax.axis_size(axis)
    initial, last = (max(0, -steps), min(count, count - steps))
    return lax.ppermute(value, axis, [(source, source + steps) for source in range(initial, last)])


def local_product(values, columns, gathered, span):
    block_size = values.shape[-1]
    tiles = gathered.reshape(-1, block_size, span)
    picked = tiles[columns]
    result = jnp.einsum("rkab,rkbw->raw", values, picked, precision=lax.Precision.HIGHEST)
    return result.reshape(-1, span)


def shards(sources, tr_vals, tr_cols, rf_vals, rf_cols):
    source_part = sources[0, 0, 0]
    trans_values = tr_vals[0, 0, 0]
    trans_index = tr_cols[0, 0, 0]
    refl_values = rf_vals[0, 0, 0]
    refl_index = rf_cols[0, 0, 0]
    piece_rows = source_part.shape[0]
    columns_total = source_part.shape[1]
    batch_count = 1
    span = columns_total // batch_count
    length = lax.axis_size("slab")
    position = lax.axis_index("slab")
    carry = jnp.zeros((piece_rows, span), jnp.float32)
    down_store = jnp.zeros_like(source_part)
    refl_store = jnp.zeros_like(source_part)
    for moment in range(length + batch_count - 1):
        incoming = passed_along(carry, "slab", 1)
        which = moment - position
        valid = (which >= 0) & (which < batch_count)
        offset = jnp.clip(which, 0, batch_count - 1) * span
        incident = incoming + source_part
        gathered = lax.all_gather(incident, "col", axis=0, tiled=True)
        trans_part = local_product(trans_values, trans_index, gathered, span)
        refl_part = local_product(refl_values, refl_index, gathered, span)
        moved, reflected = (
            lax.psum_scatter(trans_part, "row", scatter_dimension=0, tiled=True),
            lax.psum_scatter(refl_part, "row", scatter_dimension=0, tiled=True),
        )
        down_store = jnp.where(valid, moved, down_store)
        refl_store = jnp.where(valid, reflected, refl_store)
        carry = moved
    carry = jnp.zeros((piece_rows, span), jnp.float32)
    up_store = jnp.zeros_like(source_part)
    for moment in range(length + batch_count - 1):
        incoming = passed_along(carry, "slab", -1)
        which = moment - (length - 1 - position)
        valid = (which >= 0) & (which < batch_count)
        offset = jnp.clip(which, 0, batch_count - 1) * span
        incident = incoming + refl_store
        gathered = lax.all_gather(incident, "col", axis=0, tiled=True)
        trans_part = local_product(trans_values, trans_index, gathered, span)
        moved = lax.psum_scatter(trans_part, "row", scatter_dimension=0, tiled=True)
        up_store = jnp.where(valid, moved, up_store)
        carry = moved
    return (down_store + up_store)[None, None, None]


def solution(mesh):
    placed = (
        P("slab", "col", "row", None, None),
        P("slab", "col", "row", None, None, None, None),
        P("slab", "col", "row", None, None),
        P("slab", "col", "row", None, None, None, None),
        P("slab", "col", "row", None, None),
    )
    return jax.shard_map(
        shards,
        mesh=mesh,
        in_specs=placed,
        out_specs=P("slab", "col", "row", None, None),
        check_vma=False,
    )
```

profile of v0, /device:TPU:1, one launch (start us, length us, event | category | flops | bytes accessed | tf_op | source)
XLA Modules:
  0.0 898.2 jit_solution(234091020635778463)
XLA Ops:
  6.6 4.0 collective-permute-start
  10.5 7.8 collective-permute-done
  18.3 1.8 bitcast_add_fusion.3
  20.9 64.8 %all-gather.9.cloned.1.call-done = f32[6144,256]{1,0:T(8,128)} async-done(((f32[384,256]{1,0:T(8,128)}), f32[6144,256]{1,0:T(8,128)}) %all-gather.9.cloned.1.call-update) | async-done | bytes 6291472 | tf_op jit(solution)/shard_map/all_gather | solution.py:42
  85.7 10.6 %gather_fusion = f32[72,128,256]{2,1,0:T(8,128)} fusion(f32[48,128,256]{2,1,0:T(8,128)} %bitcast.155, s32[1024]{0:T(1024)S(1)} %pad_clamp_fusion.1), kind=kCustom, calls=%fused_computation | custom fusion | bytes 18874656 | tf_op jit(solution)/shard_map/gather | solution.py:16
  96.3 10.0 %fusion.22 = f32[6,256,128,1]{1,2,3,0:T(8,128)} fusion(f32[6,12,128,256]{3,2,1,0:T(8,128)} %bitcast.150, f32[1,1,1,6,12,128,128]{6,5,4,3,2,1,0:T(8,128)} %param.6), kind=kOutput, calls=%fused_computation.34 | convolution fusion | flops 3623878656 | bytes 14942208 | tf_op jit(solution)/shard_map/rkab,rkbw->raw/dot_general | solution.py:17
  106.4 11.2 %reduce-scatter.13.cloned.1.call-done = f32[384,256]{1,0:T(8,128)} async-done(((f32[768,256]{1,0:T(8,128)}), f32[384,256]{1,0:T(8,128)}) %reduce-scatter.13.cloned.1.call-update) | async-done | bytes 393232 | tf_op jit(solution)/shard_map/reduce_scatter | solution.py:46
  117.6 3.2 collective-permute-start.1
  120.8 8.6 collective-permute-done.1
  129.3 0.8 bitcast_add_fusion.2
  130.2 63.9 %all-gather.11.cloned.1.call-done = f32[6144,256]{1,0:T(8,128)} async-done(((f32[384,256]{1,0:T(8,128)}), f32[6144,256]{1,0:T(8,128)}) %all-gather.11.cloned.1.call-update) | async-done | bytes 6291472 | tf_op jit(solution)/shard_map/all_gather | solution.py:42
  194.1 10.6 %gather_fusion.1 = f32[72,128,256]{2,1,0:T(8,128)} fusion(f32[48,128,256]{2,1,0:T(8,128)} %bitcast.157, s32[1024]{0:T(1024)S(1)} %pad_clamp_fusion.1), kind=kCustom, calls=%fused_computation.1 | custom fusion | bytes 18874656 | tf_op jit(solution)/shard_map/gather | solution.py:16
  204.7 10.0 %fusion.20 = f32[6,256,128,1]{1,2,3,0:T(8,128)} fusion(f32[6,12,128,256]{3,2,1,0:T(8,128)} %bitcast.151, f32[1,1,1,6,12,128,128]{6,5,4,3,2,1,0:T(8,128)} %param.6), kind=kOutput, calls=%fused_computation.32 | convolution fusion | flops 3623878656 | bytes 14942208 | tf_op jit(solution)/shard_map/rkab,rkbw->raw/dot_general | solution.py:17
  214.7 11.2 %reduce-scatter.15.cloned.1.call-done = f32[384,256]{1,0:T(8,128)} async-done(((f32[768,256]{1,0:T(8,128)}), f32[384,256]{1,0:T(8,128)}) %reduce-scatter.15.cloned.1.call-update) | async-done | bytes 393232 | tf_op jit(solution)/shard_map/reduce_scatter | solution.py:46
  225.9 3.2 collective-permute-start.2
  229.1 8.6 collective-permute-done.2
  237.7 0.8 bitcast_add_fusion.1
  238.8 63.6 %all-gather.13.cloned.1.call-done = f32[6144,256]{1,0:T(8,128)} async-done(((f32[384,256]{1,0:T(8,128)}), f32[6144,256]{1,0:T(8,128)}) %all-gather.13.cloned.1.call-update) | async-done | bytes 6291472 | tf_op jit(solution)/shard_map/all_gather | solution.py:42
  302.4 10.6 %gather_fusion.2 = f32[72,128,256]{2,1,0:T(8,128)} fusion(f32[48,128,256]{2,1,0:T(8,128)} %bitcast.159, s32[1024]{0:T(1024)S(1)} %pad_clamp_fusion.1), kind=kCustom, calls=%fused_computation.2 | custom fusion | bytes 18874656 | tf_op jit(solution)/shard_map/gather | solution.py:16
  313.0 10.0 %fusion.18 = f32[6,256,128,1]{1,2,3,0:T(8,128)} fusion(f32[6,12,128,256]{3,2,1,0:T(8,128)} %bitcast.152, f32[1,1,1,6,12,128,128]{6,5,4,3,2,1,0:T(8,128)} %param.6), kind=kOutput, calls=%fused_computation.30 | convolution fusion | flops 3623878656 | bytes 14942208 | tf_op jit(solution)/shard_map/rkab,rkbw->raw/dot_general | solution.py:17
  323.0 11.2 %reduce-scatter.17.cloned.1.call-done = f32[384,256]{1,0:T(8,128)} async-done(((f32[768,256]{1,0:T(8,128)}), f32[384,256]{1,0:T(8,128)}) %reduce-scatter.17.cloned.1.call-update) | async-done | bytes 393232 | tf_op jit(solution)/shard_map/reduce_scatter | solution.py:46
  334.2 3.2 collective-permute-start.3
  337.4 8.6 collective-permute-done.3
  347.0 10.6 %gather_fusion.7 = f32[72,128,256]{2,1,0:T(8,128)} fusion(f32[48,128,256]{2,1,0:T(8,128)} %bitcast.156, s32[1024]{0:T(1024)S(1)} %pad_clamp_fusion), kind=kCustom, calls=%fused_computation.7 | custom fusion | bytes 18874656 | tf_op jit(solution)/shard_map/gather | solution.py:16
  357.6 10.3 %fusion = f32[6,256,128,1]{1,2,3,0:T(8,128)} fusion(f32[6,12,128,256]{3,2,1,0:T(8,128)} %bitcast.142, f32[1,1,1,6,12,128,128]{6,5,4,3,2,1,0:T(8,128)} %param.8), kind=kOutput, calls=%fused_computation.12 | convolution fusion | flops 3623878656 | bytes 14942208 | tf_op jit(solution)/shard_map/rkab,rkbw->raw/dot_general | solution.py:17
  368.3 10.6 %gather_fusion.6 = f32[72,128,256]{2,1,0:T(8,128)} fusion(f32[48,128,256]{2,1,0:T(8,128)} %bitcast.158, s32[1024]{0:T(1024)S(1)} %pad_clamp_fusion), kind=kCustom, calls=%fused_computation.6 | custom fusion | bytes 18874656 | tf_op jit(solution)/shard_map/gather | solution.py:16
  379.0 10.0 %fusion.2 = f32[6,256,128,1]{1,2,3,0:T(8,128)} fusion(f32[6,12,128,256]{3,2,1,0:T(8,128)} %bitcast.143, f32[1,1,1,6,12,128,128]{6,5,4,3,2,1,0:T(8,128)} %param.8), kind=kOutput, calls=%fused_computation.14 | convolution fusion | flops 3623878656 | bytes 14942208 | tf_op jit(solution)/shard_map/rkab,rkbw->raw/dot_general | solution.py:17
  389.0 10.8 %gather_fusion.5 = f32[72,128,256]{2,1,0:T(8,128)} fusion(f32[48,128,256]{2,1,0:T(8,128)} %bitcast.160, s32[1024]{0:T(1024)S(1)} %pad_clamp_fusion), kind=kCustom, calls=%fused_computation.5 | custom fusion | bytes 18874656 | tf_op jit(solution)/shard_map/gather | solution.py:16
  399.8 10.1 %fusion.4 = f32[6,256,128,1]{1,2,3,0:T(8,128)} fusion(f32[6,12,128,256]{3,2,1,0:T(8,128)} %bitcast.144, f32[1,1,1,6,12,128,128]{6,5,4,3,2,1,0:T(8,128)} %param.8), kind=kOutput, calls=%fused_computation.16 | convolution fusion | flops 3623878656 | bytes 14942208 | tf_op jit(solution)/shard_map/rkab,rkbw->raw/dot_general | solution.py:17
  410.7 10.6 %gather_fusion.4 = f32[72,128,256]{2,1,0:T(8,128)} fusion(f32[48,128,256]{2,1,0:T(8,128)} %bitcast.153, s32[1024]{0:T(1024)S(1)} %pad_clamp_fusion), kind=kCustom, calls=%fused_computation.4 | custom fusion | bytes 18874656 | tf_op jit(solution)/shard_map/gather | solution.py:16
  421.3 10.1 %fusion.6 = f32[6,256,128,1]{1,2,3,0:T(8,128)} fusion(f32[6,12,128,256]{3,2,1,0:T(8,128)} %bitcast.145, f32[1,1,1,6,12,128,128]{6,5,4,3,2,1,0:T(8,128)} %param.8), kind=kOutput, calls=%fused_computation.18 | convolution fusion | flops 3623878656 | bytes 14942208 | tf_op jit(solution)/shard_map/rkab,rkbw->raw/dot_general | solution.py:17
  431.5 1.3 collective-permute-start.4
  432.8 11.1 %collective-permute-done.4 = f32[384,256]{1,0:T(8,128)S(1)} collective-permute-done((f32[384,256]{1,0:T(8,128)S(1)}, f32[384,256]{1,0:T(8,128)S(1)}, u32[]{:S(2)}, u32[]{:S(2)}) %collective-permute-start.4) | collective-permute-done | bytes 393248 | tf_op jit(solution)/shard_map/ppermute | solution.py:10
  443.9 9.1 %reduce-scatter.23.cloned.1.call-done = f32[384,256]{1,0:T(8,128)} async-done(((f32[768,256]{1,0:T(8,128)}), f32[384,256]{1,0:T(8,128)}) %reduce-scatter.23.cloned.1.call-update) | async-done | bytes 393232 | tf_op jit(solution)/shard_map/reduce_scatter | solution.py:47
  453.1 14.5 %reduce-scatter.21.cloned.1.call-done = f32[384,256]{1,0:T(8,128)} async-done(((f32[768,256]{1,0:T(8,128)}), f32[384,256]{1,0:T(8,128)}) %reduce-scatter.21.cloned.1.call-update) | async-done | bytes 393232 | tf_op jit(solution)/shard_map/reduce_scatter | solution.py:47
  467.6 1.9 fusion.26
  469.6 62.2 %all-gather.17.cloned.1.call-done = f32[6144,256]{1,0:T(8,128)} async-done(((f32[384,256]{1,0:T(8,128)}), f32[6144,256]{1,0:T(8,128)}) %all-gather.17.cloned.1.call-update) | async-done | bytes 6291472 | tf_op jit(solution)/shard_map/all_gather | solution.py:60
  531.7 10.6 %gather_fusion.8 = f32[72,128,256]{2,1,0:T(8,128)} fusion(f32[48,128,256]{2,1,0:T(8,128)} %bitcast.162, s32[1024]{0:T(1024)S(1)} %pad_clamp_fusion.1), kind=kCustom, calls=%fused_computation.8 | custom fusion | bytes 18874656 | tf_op jit(solution)/shard_map/gather | solution.py:16
  542.3 10.0 %fusion.14 = f32[6,256,128,1]{1,2,3,0:T(8,128)} fusion(f32[6,12,128,256]{3,2,1,0:T(8,128)} %bitcast.146, f32[1,1,1,6,12,128,128]{6,5,4,3,2,1,0:T(8,128)} %param.6), kind=kOutput, calls=%fused_computation.26 | convolution fusion | flops 3623878656 | bytes 14942208 | tf_op jit(solution)/shard_map/rkab,rkbw->raw/dot_general | solution.py:17
  552.4 11.2 %reduce-scatter.29.cloned.1.call-done = f32[384,256]{1,0:T(8,128)} async-done(((f32[768,256]{1,0:T(8,128)}), f32[384,256]{1,0:T(8,128)}) %reduce-scatter.29.cloned.1.call-update) | async-done | bytes 393232 | tf_op jit(solution)/shard_map/reduce_scatter | solution.py:62
  563.5 1.3 collective-permute-start.5
  564.8 11.3 %collective-permute-done.5 = f32[384,256]{1,0:T(8,128)S(1)} collective-permute-done((f32[384,256]{1,0:T(8,128)}, f32[384,256]{1,0:T(8,128)S(1)}, u32[]{:S(2)}, u32[]{:S(2)}) %collective-permute-start.5) | collective-permute-done | bytes 393248 | tf_op jit(solution)/shard_map/ppermute | solution.py:10
  576.2 0.8 add.88
  577.3 62.8 %all-gather.19.cloned.1.call-done = f32[6144,256]{1,0:T(8,128)} async-done(((f32[384,256]{1,0:T(8,128)}), f32[6144,256]{1,0:T(8,128)}) %all-gather.19.cloned.1.call-update) | async-done | bytes 6291472 | tf_op jit(solution)/shard_map/all_gather | solution.py:60
  640.1 10.6 %gather_fusion.9 = f32[72,128,256]{2,1,0:T(8,128)} fusion(f32[48,128,256]{2,1,0:T(8,128)} %bitcast.163, s32[1024]{0:T(1024)S(1)} %pad_clamp_fusion.1), kind=kCustom, calls=%fused_computation.9 | custom fusion | bytes 18874656 | tf_op jit(solution)/shard_map/gather | solution.py:16
  650.6 10.0 %fusion.12 = f32[6,256,128,1]{1,2,3,0:T(8,128)} fusion(f32[6,12,128,256]{3,2,1,0:T(8,128)} %bitcast.147, f32[1,1,1,6,12,128,128]{6,5,4,3,2,1,0:T(8,128)} %param.6), kind=kOutput, calls=%fused_computation.24 | convolution fusion | flops 3623878656 | bytes 14942208 | tf_op jit(solution)/shard_map/rkab,rkbw->raw/dot_general | solution.py:17
  660.7 11.2 %reduce-scatter.31.cloned.1.call-done = f32[384,256]{1,0:T(8,128)} async-done(((f32[768,256]{1,0:T(8,128)}), f32[384,256]{1,0:T(8,128)}) %reduce-scatter.31.cloned.1.call-update) | async-done | bytes 393232 | tf_op jit(solution)/shard_map/reduce_scatter | solution.py:62
  671.9 1.3 collective-permute-start.6
  673.2 11.3 %collective-permute-done.6 = f32[384,256]{1,0:T(8,128)S(1)} collective-permute-done((f32[384,256]{1,0:T(8,128)}, f32[384,256]{1,0:T(8,128)S(1)}, u32[]{:S(2)}, u32[]{:S(2)}) %collective-permute-start.6) | collective-permute-done | bytes 393248 | tf_op jit(solution)/shard_map/ppermute | solution.py:10
  684.5 0.8 add.89
  685.3 63.0 %all-gather.21.cloned.1.call-done = f32[6144,256]{1,0:T(8,128)} async-done(((f32[384,256]{1,0:T(8,128)}), f32[6144,256]{1,0:T(8,128)}) %all-gather.21.cloned.1.call-update) | async-done | bytes 6291472 | tf_op jit(solution)/shard_map/all_gather | solution.py:60
  748.4 10.6 %gather_fusion.10 = f32[72,128,256]{2,1,0:T(8,128)} fusion(f32[48,128,256]{2,1,0:T(8,128)} %bitcast.164, s32[1024]{0:T(1024)S(1)} %pad_clamp_fusion.1), kind=kCustom, calls=%fused_computation.10 | custom fusion | bytes 18874656 | tf_op jit(solution)/shard_map/gather | solution.py:16
  759.0 10.0 %fusion.10 = f32[6,256,128,1]{1,2,3,0:T(8,128)} fusion(f32[6,12,128,256]{3,2,1,0:T(8,128)} %bitcast.148, f32[1,1,1,6,12,128,128]{6,5,4,3,2,1,0:T(8,128)} %param.6), kind=kOutput, calls=%fused_computation.22 | convolution fusion | flops 3623878656 | bytes 14942208 | tf_op jit(solution)/shard_map/rkab,rkbw->raw/dot_general | solution.py:17
  769.0 11.2 %reduce-scatter.33.cloned.1.call-done = f32[384,256]{1,0:T(8,128)} async-done(((f32[768,256]{1,0:T(8,128)}), f32[384,256]{1,0:T(8,128)}) %reduce-scatter.33.cloned.1.call-update) | async-done | bytes 393232 | tf_op jit(solution)/shard_map/reduce_scatter | solution.py:62
  780.2 1.3 collective-permute-start.7
  781.5 11.3 %collective-permute-done.7 = f32[384,256]{1,0:T(8,128)S(1)} collective-permute-done((f32[384,256]{1,0:T(8,128)}, f32[384,256]{1,0:T(8,128)S(1)}, u32[]{:S(2)}, u32[]{:S(2)}) %collective-permute-start.7) | collective-permute-done | bytes 393248 | tf_op jit(solution)/shard_map/ppermute | solution.py:10
  792.8 0.8 add.90
  794.0 10.6 %gather_fusion.3 = f32[72,128,256]{2,1,0:T(8,128)} fusion(f32[48,128,256]{2,1,0:T(8,128)} %bitcast.154, s32[1024]{0:T(1024)S(1)} %pad_clamp_fusion.1), kind=kCustom, calls=%fused_computation.3 | custom fusion | bytes 18874656 | tf_op jit(solution)/shard_map/gather | solution.py:16
  804.5 10.3 %fusion.16 = f32[6,256,128,1]{1,2,3,0:T(8,128)} fusion(f32[6,12,128,256]{3,2,1,0:T(8,128)} %bitcast.149, f32[1,1,1,6,12,128,128]{6,5,4,3,2,1,0:T(8,128)} %param.6), kind=kOutput, calls=%fused_computation.28 | convolution fusion | flops 3623878656 | bytes 14942208 | tf_op jit(solution)/shard_map/rkab,rkbw->raw/dot_general | solution.py:17
  814.9 41.8 %all-gather.23.cloned.1.call-done = f32[6144,256]{1,0:T(8,128)} async-done(((f32[384,256]{1,0:T(8,128)}), f32[6144,256]{1,0:T(8,128)}) %all-gather.23.cloned.1.call-update) | async-done | bytes 6291472 | tf_op jit(solution)/shard_map/all_gather | solution.py:60
  856.7 10.6 %gather_fusion.11 = f32[72,128,256]{2,1,0:T(8,128)} fusion(f32[48,128,256]{2,1,0:T(8,128)} %bitcast.161, s32[1024]{0:T(1024)S(1)} %pad_clamp_fusion.1), kind=kCustom, calls=%fused_computation.11 | custom fusion | bytes 18874656 | tf_op jit(solution)/shard_map/gather | solution.py:16
  867.3 10.3 %fusion.8 = f32[6,256,128,1]{1,2,3,0:T(8,128)} fusion(f32[6,12,128,256]{3,2,1,0:T(8,128)} %bitcast.141, f32[1,1,1,6,12,128,128]{6,5,4,3,2,1,0:T(8,128)} %param.6), kind=kOutput, calls=%fused_computation.20 | convolution fusion | flops 3623878656 | bytes 14942208 | tf_op jit(solution)/shard_map/rkab,rkbw->raw/dot_general | solution.py:17
  877.7 11.3 %reduce-scatter.35.cloned.1.call-done = f32[384,256]{1,0:T(8,128)} async-done(((f32[768,256]{1,0:T(8,128)}), f32[384,256]{1,0:T(8,128)}) %reduce-scatter.35.cloned.1.call-update) | async-done | bytes 393232 | tf_op jit(solution)/shard_map/reduce_scatter | solution.py:62
  889.0 2.0 add_bitcast_fusion
  (68 shorter events, 4.7 us)
Async XLA Ops:
  6.5 79.2 %all-gather.9.cloned.1.call-start = ((), (), s32[]{:S(2)}) async-start(), calls=%async_computation.12 | async-start | bytes 6684672 | tf_op jit(solution)/shard_map/all_gather | solution.py:42
  6.6 11.7 %collective-permute-start = (f32[384,256]{1,0:T(8,128)S(1)}, f32[384,256]{1,0:T(8,128)S(1)}, u32[]{:S(2)}, u32[]{:S(2)}) collective-permute-start(f32[384,256]{1,0:T(8,128)S(1)} %broadcast.37), channel_id=1, source_target_pairs={{0,32},{32,64},{64,96},{1,33},{33,65},{65,97},{2,34},{34,66},{66,9... | collective-permute-start | bytes 1179656 | tf_op jit(solution)/shard_map/ppermute | solution.py:10
  20.1 97.5 %reduce-scatter.13.cloned.1.call-start = ((), (), s32[]{:S(2)}) async-start(), calls=%async_computation.13 | async-start | bytes 1179648 | tf_op jit(solution)/shard_map/reduce_scatter | solution.py:46
  96.3 33.1 %copy-start = (f32[1,1,1,384,256]{4,3,2,1,0:T(8,128)S(1)}, f32[1,1,1,384,256]{4,3,2,1,0:T(8,128)}, u32[]{:S(2)}) copy-start(f32[1,1,1,384,256]{4,3,2,1,0:T(8,128)} %param.5) | copy-start | bytes 1179652
  106.3 87.8 %all-gather.11.cloned.1.call-start = ((), (), s32[]{:S(2)}) async-start(), calls=%async_computation.14 | async-start | bytes 6684672 | tf_op jit(solution)/shard_map/all_gather | solution.py:42
  117.6 11.8 %collective-permute-start.1 = (f32[384,256]{1,0:T(8,128)}, f32[384,256]{1,0:T(8,128)S(1)}, u32[]{:S(2)}, u32[]{:S(2)}) collective-permute-start(f32[384,256]{1,0:T(8,128)} %reduce-scatter.13.cloned.1.call-done), channel_id=1, source_target_pairs={{0,32},{32,64},{64,96},{1,33},{33,65},{65,97},{2,34},{34,66},{66,9... | collective-permute-start | bytes 1179656 | tf_op jit(solution)/shard_map/ppermute | solution.py:10
  130.2 95.7 %reduce-scatter.15.cloned.1.call-start = ((), (), s32[]{:S(2)}) async-start(), calls=%async_computation.15 | async-start | bytes 1179648 | tf_op jit(solution)/shard_map/reduce_scatter | solution.py:46
  214.7 87.7 %all-gather.13.cloned.1.call-start = ((), (), s32[]{:S(2)}) async-start(), calls=%async_computation.16 | async-start | bytes 6684672 | tf_op jit(solution)/shard_map/all_gather | solution.py:42
  225.9 11.8 %collective-permute-start.2 = (f32[384,256]{1,0:T(8,128)}, f32[384,256]{1,0:T(8,128)S(1)}, u32[]{:S(2)}, u32[]{:S(2)}) collective-permute-start(f32[384,256]{1,0:T(8,128)} %reduce-scatter.15.cloned.1.call-done), channel_id=1, source_target_pairs={{0,32},{32,64},{64,96},{1,33},{33,65},{65,97},{2,34},{34,66},{66,9... | collective-permute-start | bytes 1179656 | tf_op jit(solution)/shard_map/ppermute | solution.py:10
  238.5 95.7 %reduce-scatter.17.cloned.1.call-start = ((), (), s32[]{:S(2)}) async-start(), calls=%async_computation.17 | async-start | bytes 1179648 | tf_op jit(solution)/shard_map/reduce_scatter | solution.py:46
  313.0 33.9 %copy-start.7 = (s32[1,1,1,6,12]{4,2,3,1,0:T(1,128)S(1)}, s32[1,1,1,6,12]{4,2,3,1,0:T(1,128)}, u32[]{:S(2)}) copy-start(s32[1,1,1,6,12]{4,2,3,1,0:T(1,128)} %param.9) | copy-start | bytes 868
  323.0 87.8 %all-gather.15.cloned.1.call-start = ((), (), s32[]{:S(2)}) async-start(), calls=%async_computation.18 | async-start | bytes 6684672 | tf_op jit(solution)/shard_map/all_gather | solution.py:42
  334.2 11.8 %collective-permute-start.3 = (f32[384,256]{1,0:T(8,128)}, f32[384,256]{1,0:T(8,128)S(1)}, u32[]{:S(2)}, u32[]{:S(2)}) collective-permute-start(f32[384,256]{1,0:T(8,128)} %reduce-scatter.17.cloned.1.call-done), channel_id=1, source_target_pairs={{0,32},{32,64},{64,96},{1,33},{33,65},{65,97},{2,34},{34,66},{66,9... | collective-permute-start | bytes 1179656 | tf_op jit(solution)/shard_map/ppermute | solution.py:10
  346.8 97.1 %reduce-scatter.27.cloned.1.call-start = ((), (), s32[]{:S(2)}) async-start(), calls=%async_computation.23 | async-start | bytes 1179648 | tf_op jit(solution)/shard_map/reduce_scatter | solution.py:47
  367.9 76.1 %reduce-scatter.25.cloned.1.call-start = ((), (), s32[]{:S(2)}) async-start(), calls=%async_computation.22 | async-start | bytes 1179648 | tf_op jit(solution)/shard_map/reduce_scatter | solution.py:47
  389.0 64.1 %reduce-scatter.23.cloned.1.call-start = ((), (), s32[]{:S(2)}) async-start(), calls=%async_computation.21 | async-start | bytes 1179648 | tf_op jit(solution)/shard_map/reduce_scatter | solution.py:47
  410.0 57.6 %reduce-scatter.21.cloned.1.call-start = ((), (), s32[]{:S(2)}) async-start(), calls=%async_computation.20 | async-start | bytes 1179648 | tf_op jit(solution)/shard_map/reduce_scatter | solution.py:47
  431.5 100.3 %all-gather.17.cloned.1.call-start = ((), (), s32[]{:S(2)}) async-start(), calls=%async_computation.24 | async-start | bytes 6684672 | tf_op jit(solution)/shard_map/all_gather | solution.py:60
  431.5 12.4 %collective-permute-start.4 = (f32[384,256]{1,0:T(8,128)S(1)}, f32[384,256]{1,0:T(8,128)S(1)}, u32[]{:S(2)}, u32[]{:S(2)}) collective-permute-start(f32[384,256]{1,0:T(8,128)S(1)} %broadcast.37), channel_id=1, source_target_pairs={{32,0},{64,32},{96,64},{33,1},{65,33},{97,65},{34,2},{66,34},{98,6... | collective-permute-start | bytes 1179656 | tf_op jit(solution)/shard_map/ppermute | solution.py:10
  469.5 94.0 %reduce-scatter.29.cloned.1.call-start = ((), (), s32[]{:S(2)}) async-start(), calls=%async_computation.25 | async-start | bytes 1179648 | tf_op jit(solution)/shard_map/reduce_scatter | solution.py:62
  552.3 87.8 %all-gather.19.cloned.1.call-start = ((), (), s32[]{:S(2)}) async-start(), calls=%async_computation.26 | async-start | bytes 6684672 | tf_op jit(solution)/shard_map/all_gather | solution.py:60
  563.5 12.6 %collective-permute-start.5 = (f32[384,256]{1,0:T(8,128)}, f32[384,256]{1,0:T(8,128)S(1)}, u32[]{:S(2)}, u32[]{:S(2)}) collective-permute-start(f32[384,256]{1,0:T(8,128)} %reduce-scatter.29.cloned.1.call-done), channel_id=1, source_target_pairs={{32,0},{64,32},{96,64},{33,1},{65,33},{97,65},{34,2},{66,34},{98,6... | collective-permute-start | bytes 1179656 | tf_op jit(solution)/shard_map/ppermute | solution.py:10
  577.0 94.9 %reduce-scatter.31.cloned.1.call-start = ((), (), s32[]{:S(2)}) async-start(), calls=%async_computation.27 | async-start | bytes 1179648 | tf_op jit(solution)/shard_map/reduce_scatter | solution.py:62
  660.7 87.7 %all-gather.21.cloned.1.call-start = ((), (), s32[]{:S(2)}) async-start(), calls=%async_computation.28 | async-start | bytes 6684672 | tf_op jit(solution)/shard_map/all_gather | solution.py:60
  671.9 12.6 %collective-permute-start.6 = (f32[384,256]{1,0:T(8,128)}, f32[384,256]{1,0:T(8,128)S(1)}, u32[]{:S(2)}, u32[]{:S(2)}) collective-permute-start(f32[384,256]{1,0:T(8,128)} %reduce-scatter.31.cloned.1.call-done), channel_id=1, source_target_pairs={{32,0},{64,32},{96,64},{33,1},{65,33},{97,65},{34,2},{66,34},{98,6... | collective-permute-start | bytes 1179656 | tf_op jit(solution)/shard_map/ppermute | solution.py:10
  685.3 94.9 %reduce-scatter.33.cloned.1.call-start = ((), (), s32[]{:S(2)}) async-start(), calls=%async_computation.29 | async-start | bytes 1179648 | tf_op jit(solution)/shard_map/reduce_scatter | solution.py:62
  769.0 87.7 %all-gather.23.cloned.1.call-start = ((), (), s32[]{:S(2)}) async-start(), calls=%async_computation.30 | async-start | bytes 6684672 | tf_op jit(solution)/shard_map/all_gather | solution.py:60
  780.2 12.6 %collective-permute-start.7 = (f32[384,256]{1,0:T(8,128)}, f32[384,256]{1,0:T(8,128)S(1)}, u32[]{:S(2)}, u32[]{:S(2)}) collective-permute-start(f32[384,256]{1,0:T(8,128)} %reduce-scatter.33.cloned.1.call-done), channel_id=1, source_target_pairs={{32,0},{64,32},{96,64},{33,1},{65,33},{97,65},{34,2},{66,34},{98,6... | collective-permute-start | bytes 1179656 | tf_op jit(solution)/shard_map/ppermute | solution.py:10
  793.7 84.0 %reduce-scatter.19.cloned.1.call-start = ((), (), s32[]{:S(2)}) async-start(), calls=%async_computation.19 | async-start | bytes 1179648 | tf_op jit(solution)/shard_map/reduce_scatter | solution.py:46
  814.9 74.1 %reduce-scatter.35.cloned.1.call-start = ((), (), s32[]{:S(2)}) async-start(), calls=%async_computation.31 | async-start | bytes 1179648 | tf_op jit(solution)/shard_map/reduce_scatter | solution.py:62
  867.3 21.7 %copy-start.1 = (f32[384,256]{1,0:T(8,128)S(1)}, f32[384,256]{1,0:T(8,128)}, u32[]{:S(2)}) copy-start(f32[384,256]{1,0:T(8,128)} %reduce-scatter.13.cloned.1.call-done) | copy-start | bytes 1179652
  867.3 21.7 %copy-start.2 = (f32[384,256]{1,0:T(8,128)S(1)}, f32[384,256]{1,0:T(8,128)}, u32[]{:S(2)}) copy-start(f32[384,256]{1,0:T(8,128)} %reduce-scatter.15.cloned.1.call-done) | copy-start | bytes 1179652
  867.3 21.7 %copy-start.3 = (f32[384,256]{1,0:T(8,128)S(1)}, f32[384,256]{1,0:T(8,128)}, u32[]{:S(2)}) copy-start(f32[384,256]{1,0:T(8,128)} %reduce-scatter.17.cloned.1.call-done) | copy-start | bytes 1179652
  867.3 21.7 %copy-start.4 = (f32[384,256]{1,0:T(8,128)S(1)}, f32[384,256]{1,0:T(8,128)}, u32[]{:S(2)}) copy-start(f32[384,256]{1,0:T(8,128)} %reduce-scatter.29.cloned.1.call-done) | copy-start | bytes 1179652
  867.3 21.7 %copy-start.5 = (f32[384,256]{1,0:T(8,128)S(1)}, f32[384,256]{1,0:T(8,128)}, u32[]{:S(2)}) copy-start(f32[384,256]{1,0:T(8,128)} %reduce-scatter.31.cloned.1.call-done) | copy-start | bytes 1179652
  867.3 21.7 %copy-start.6 = (f32[384,256]{1,0:T(8,128)S(1)}, f32[384,256]{1,0:T(8,128)}, u32[]{:S(2)}) copy-start(f32[384,256]{1,0:T(8,128)} %reduce-scatter.33.cloned.1.call-done) | copy-start | bytes 1179652
Sparse Core Ops, SparseCore 0:
  20.2 65.4 all-gather.8
  106.5 11.0 reduce-scatter.12
  130.3 63.7 all-gather.10
  214.8 11.0 reduce-scatter.14
  238.6 63.7 all-gather.12
  323.1 11.0 reduce-scatter.16
  346.9 63.7 all-gather.14
  413.1 11.0 reduce-scatter.26
  426.5 12.1 reduce-scatter.24
  440.9 12.1 reduce-scatter.22
  455.5 12.1 reduce-scatter.20
  469.6 62.0 all-gather.16
  552.4 11.0 reduce-scatter.28
  577.1 62.9 all-gather.18
  660.8 11.0 reduce-scatter.30
  685.4 62.9 all-gather.20
  769.1 11.0 reduce-scatter.32
  793.8 62.8 all-gather.22
  859.0 11.0 reduce-scatter.18
  877.7 11.1 reduce-scatter.34
where the time goes:
time: 907 us; the launch traced here: 898 us
  waiting for transfers between devices  604 us (67%)
  local copies, waits for them, and re-layouts  127 us (14%)
  matrix products  121 us (13%)
  starting transfers between devices  20.7 us (2%)
  between operations  14.3 us (2%)
  other arithmetic  11.1 us (1%)
    all_gather x8, waiting for transfers between devices, shards(): gathered = lax.all_gather(incident, 'col', axis=0, tiled=True)  423 us
    gather x12, local copies, waits for them, and re-layouts, local_product(): picked = tiles[columns]  127 us
    dot_general x12, matrix products, local_product(): jnp.einsum('rkab,rkbw->raw', values, picked, precision=lax.Precision.HIGH...  121 us
    ppermute x8, waiting for transfers between devices, passed_along(): lax.ppermute(value, axis, [(source, source + steps) for source in range(i...  78.6 us
    reduce_scatter x4, waiting for transfers between devices, shards(): moved = lax.psum_scatter(trans_part, 'row', scatter_dimension=0, tiled=True)  44.8 us
    reduce_scatter x4, waiting for transfers between devices, shards(): lax.psum_scatter(trans_part, 'row', scatter_dimension=0, tiled=True)  33.5 us
    reduce_scatter x4, waiting for transfers between devices, shards(): lax.psum_scatter(refl_part, 'row', scatter_dimension=0, tiled=True)  23.7 us
    ppermute x8, starting transfers between devices, passed_along(): lax.ppermute(value, axis, [(source, source + steps) for source in range(i...  18.7 us
  transfers between devices with their start and end apart: 28, of which 25 were waited for; matrix products, arithmetic and copies ran while one was open for 14% of the time, Pallas kernels for 0%

commit v1 on v0

v1 whole, which is shorter than its diff:
```python
import functools

import jax
import jax.numpy as jnp
from jax import lax
from jax.experimental import pallas as pl
from jax.experimental.pallas import tpu as pltpu
from jax.sharding import PartitionSpec as P

MESH = pl.DeviceIdType.MESH
BATCHES = 8
STAGE = 5
TURN = 5
RING = 4
PIECES = RING * RING
BLOCK = 128


def kernel(
    dims,
    src_ref,
    trv_ref,
    rfv_ref,
    trc_ref,
    rfc_ref,
    out_ref,
    gat,
    xs,
    wts,
    stage,
    src_t,
    xrecv,
    down_s,
    refl_s,
    up_s,
    own,
    ex_src,
    ex_dst,
    cols,
    load_sem,
    tree_recv,
    tree_send,
    ex_recv,
    ex_send,
    x_recv,
    x_send,
):
    batches, width, blocks, row_blocks, picks, slabs = dims
    rows = blocks * width
    half = rows // 2
    own_rows = row_blocks // 2
    s = lax.axis_index("slab")
    r = lax.axis_index("row")
    c = lax.axis_index("col")
    y = lax.rem(c, RING)
    z = lax.div(c, RING)
    a = y * (1 - r) + z * r
    b = z * (1 - r) + y * r
    step_a = 1 + (RING - 1) * r
    step_b = RING - (RING - 1) * r

    def col(da, db):
        return lax.rem(a + da + RING, RING) * step_a + lax.rem(b + db + RING, RING) * step_b

    def plane(da, db):
        return (s, r, col(da, db))

    partner = (s, 1 - r, c)
    below = (lax.rem(s + 1, slabs), r, c)
    above = (lax.rem(s + slabs - 1, slabs), r, c)

    def load(op, i):
        ref = trv_ref if op == 0 else rfv_ref
        return pltpu.make_async_copy(ref.at[i], stage.at[op * row_blocks + i], load_sem.at[op * row_blocks + i])

    for op in range(2):
        for i in range(row_blocks):
            load(op, i).start()

    barrier = pltpu.get_barrier_semaphore()
    greeted = (plane(1, 0), plane(-1, 0), plane(0, 1), plane(0, -1), partner, below, above)
    for device in greeted:
        pl.semaphore_signal(barrier, inc=1, device_id=device, device_id_type=MESH)

    for i in range(row_blocks):
        for k in range(picks):
            cols[0, i, k] = trc_ref[i, k]
            cols[1, i, k] = rfc_ref[i, k]
    for j in range(blocks):
        turned = jnp.transpose(src_ref[j * BLOCK : (j + 1) * BLOCK, :])
        for n in range(batches):
            src_t[n, j * width : (j + 1) * width, :] = turned[n * width : (n + 1) * width, :]

    pl.semaphore_wait(barrier, len(greeted))

    def tree(n, piece, part, device, group):
        where = gat.at[n, piece] if part is None else gat.at[n, piece, pl.ds(part * half, half)]
        pltpu.make_async_remote_copy(
            src_ref=where,
            dst_ref=where,
            send_sem=tree_send.at[n],
            recv_sem=tree_recv.at[n, group],
            device_id=device,
            device_id_type=MESH,
        ).start()

    def tree_wait(n, group, count):
        some = gat.at[n, pl.ds(0, count)]
        pltpu.make_async_copy(some, some, tree_recv.at[n, group]).wait()

    def both_sides(n, piece, group):
        tree(n, piece, None, plane(0, 1), group)
        tree(n, piece, None, plane(0, -1), group)

    def halves(n, da):
        tree(n, col(da, -1), 0, plane(0, 1), 5)
        tree(n, col(da, 1), 1, plane(0, -1), 5)

    def x_copy(source, n, device):
        return pltpu.make_async_remote_copy(
            src_ref=source,
            dst_ref=xrecv.at[n],
            send_sem=x_send.at[n],
            recv_sem=x_recv.at[n],
            device_id=device,
            device_id_type=MESH,
        )

    def inject(n, batch, is_down):
        @pl.when(is_down & (s == 0))
        def _():
            gat[n, c] = src_t[batch]

        @pl.when(jnp.logical_not(is_down) & (s == slabs - 1))
        def _():
            gat[n, c] = refl_s[batch]

        @pl.when(is_down & (s > 0))
        def _():
            x_copy(xrecv.at[n], n, above).wait_recv()
            gat[n, c] = src_t[batch] + xrecv[n]

        @pl.when(jnp.logical_not(is_down) & (s < slabs - 1))
        def _():
            x_copy(xrecv.at[n], n, above).wait_recv()
            gat[n, c] = refl_s[batch] + xrecv[n]

        tree(n, c, None, plane(1, 0), 0)
        tree(n, c, None, plane(-1, 0), 0)
        both_sides(n, c, 2)

    def relay_1(n, batch, is_down):
        tree_wait(n, 0, 2)
        tree(n, col(-1, 0), 0, plane(1, 0), 1)
        tree(n, col(1, 0), 1, plane(-1, 0), 1)
        both_sides(n, col(-1, 0), 3)
        both_sides(n, col(1, 0), 3)
        tree_wait(n, 2, 2)
        halves(n, 0)

    def relay_2(n, batch, is_down):
        tree_wait(n, 1, 1)
        both_sides(n, col(2, 0), 4)
        tree_wait(n, 3, 4)
        halves(n, -1)
        halves(n, 1)

    def relay_3(n, batch, is_down):
        tree_wait(n, 4, 2)
        halves(n, 2)

    def prepare(item, carry):
        pltpu.make_async_copy(trv_ref.at[0], stage.at[item], load_sem.at[item]).wait()
        for k in range(picks):
            value = stage[item, k]
            high = value.astype(jnp.bfloat16)
            low = (value - high.astype(jnp.float32)).astype(jnp.bfloat16)
            wts[item, 0:BLOCK, k * BLOCK : (k + 1) * BLOCK] = high
            wts[item, BLOCK : 2 * BLOCK, k * BLOCK : (k + 1) * BLOCK] = low
        return carry

    def ex_copy(n, op):
        return pltpu.make_async_remote_copy(
            src_ref=ex_src.at[n, op],
            dst_ref=ex_dst.at[n, op],
            send_sem=ex_send.at[n, op],
            recv_sem=ex_recv.at[n, op],
            device_id=partner,
            device_id_type=MESH,
        )

    def product(op, i):
        picked = jnp.concatenate([xs[cols[op, i, k]] for k in range(picks)], axis=1)
        full = lax.dot_general(
            picked,
            wts[op * row_blocks + i],
            (((1,), (1,)), ((), ())),
            preferred_element_type=jnp.float32,
        )
        high, low = full[:width], full[width:]
        return high[:, :BLOCK] + ((high[:, BLOCK:] + low[:, :BLOCK]) + low[:, BLOCK:])

    def apply(n, op):
        for j in range(own_rows):
            ex_src[n, op, j * width : (j + 1) * width, :] = product(op, (1 - r) * own_rows + j)
        ex_copy(n, op).start()
        for j in range(own_rows):
            own[op, j * width : (j + 1) * width, :] = product(op, r * own_rows + j)

    def finish(n, batch, is_down):
        tree_wait(n, 5, RING)
        for p in range(PIECES):
            for j in range(blocks):
                value = gat[n, p, j * width : (j + 1) * width, :]
                high = value.astype(jnp.bfloat16)
                xs[p * blocks + j, 0:width, :] = high
                xs[p * blocks + j, width : 2 * width, :] = (value - high.astype(jnp.float32)).astype(jnp.bfloat16)
        apply(n, 0)

        @pl.when(is_down)
        def _():
            apply(n, 1)
            ex_copy(n, 0).wait_recv()
            down_s[batch] = own[0] + ex_dst[n, 0]

            @pl.when(s < slabs - 1)
            def _():
                x_copy(down_s.at[batch], n, below).start()

            ex_copy(n, 1).wait_recv()
            refl_s[batch] = own[1] + ex_dst[n, 1]

        @pl.when(jnp.logical_not(is_down))
        def _():
            ex_copy(n, 0).wait_recv()
            up_s[batch] = own[0] + ex_dst[n, 0]

            @pl.when(s > 0)
            def _():
                x_copy(up_s.at[batch], n, above).start()

            out_ref[batch] = down_s[batch] + up_s[batch]

    offset = (2 * (slabs - 1) - 2 * s) * STAGE + TURN

    def phase(body, slot, delay, first=0):
        at = slot - delay + 2 * batches
        is_down = lax.rem(at, 2) == 0
        batch = jnp.where(is_down, lax.div(at, 2) - batches, lax.div(at - offset + 64, 2) - batches - 32)
        valid = (batch >= 0) & (batch < batches)

        @pl.when(valid)
        def _():
            body(jnp.where(is_down, batch, batches + batch), batch, is_down)

    items = 2 * row_blocks
    each = 3

    @pl.when(s > 0)
    def _():
        lax.fori_loop(0, items, prepare, 0)

    def slot_body(slot, carry):
        phase(relay_3, slot, 3)
        phase(relay_2, slot, 2)
        phase(relay_1, slot, 1)
        phase(inject, slot, 0)

        @pl.when((s == 0) & (slot < items // each))
        def _():
            lax.fori_loop(slot * each, slot * each + each, prepare, 0)

        phase(finish, slot, 4)
        return carry

    lax.fori_loop(0, 2 * (batches - 1) + offset + 5, slot_body, 0)

    def drain(n, carry):
        sent = gat.at[n, pl.ds(0, PIECES - 1)]
        pltpu.make_async_copy(sent, sent, tree_send.at[n]).wait()
        ex_copy(n, 0).wait_send()

        @pl.when(n < batches)
        def _():
            ex_copy(n, 1).wait_send()

        @pl.when(((n < batches) & (s < slabs - 1)) | ((n >= batches) & (s > 0)))
        def _():
            x_copy(up_s.at[0], n, above).wait_send()

        return carry

    lax.fori_loop(0, 2 * batches, drain, 0)


def shards(slabs, sources, tr_vals, tr_cols, rf_vals, rf_cols):
    source = sources[0, 0, 0]
    rows_in, span = source.shape
    row_blocks, picks = tr_cols.shape[-2:]
    blocks = rows_in // BLOCK
    batches = BATCHES
    width = span // batches
    rows = blocks * width
    tasks = 2 * batches
    f32, bf16 = jnp.float32, jnp.bfloat16
    vmem = pl.BlockSpec(memory_space=pltpu.VMEM)
    smem = pl.BlockSpec(memory_space=pltpu.SMEM)
    hbm = pl.BlockSpec(memory_space=pl.ANY)
    dma = pltpu.SemaphoreType.DMA
    out = pl.pallas_call(
        functools.partial(kernel, (batches, width, blocks, row_blocks, picks, slabs)),
        out_shape=jax.ShapeDtypeStruct((batches, rows, BLOCK), f32),
        in_specs=[vmem, hbm, hbm, smem, smem],
        out_specs=vmem,
        scratch_shapes=[
            pltpu.VMEM((tasks, PIECES, rows, BLOCK), f32),
            pltpu.VMEM((PIECES * blocks, 2 * width, BLOCK), bf16),
            pltpu.VMEM((2 * row_blocks, 2 * BLOCK, picks * BLOCK), bf16),
            pltpu.VMEM((2 * row_blocks, picks, BLOCK, BLOCK), f32),
            pltpu.VMEM((batches, rows, BLOCK), f32),
            pltpu.VMEM((tasks, rows, BLOCK), f32),
            pltpu.VMEM((batches, rows, BLOCK), f32),
            pltpu.VMEM((batches, rows, BLOCK), f32),
            pltpu.VMEM((batches, rows, BLOCK), f32),
            pltpu.VMEM((2, rows, BLOCK), f32),
            pltpu.VMEM((tasks, 2, rows, BLOCK), f32),
            pltpu.VMEM((tasks, 2, rows, BLOCK), f32),
            pltpu.SMEM((2, row_blocks, picks), jnp.int32),
            dma((2 * row_blocks,)),
            dma((tasks, 6)),
            dma((tasks,)),
            dma((tasks, 2)),
            dma((tasks, 2)),
            dma((tasks,)),
            dma((tasks,)),
        ],
        compiler_params=pltpu.CompilerParams(
            collective_id=0,
            has_side_effects=True,
            vmem_limit_bytes=60 * 1024 * 1024,
        ),
    )(source, tr_vals[0, 0, 0], rf_vals[0, 0, 0], tr_cols[0, 0, 0], rf_cols[0, 0, 0])
    out = out.reshape(batches, blocks, width, BLOCK).transpose(1, 3, 0, 2)
    return out.reshape(rows_in, span)[None, None, None]


def solution(mesh):
    placed = (
        P("slab", "col", "row", None, None),
        P("slab", "col", "row", None, None, None, None),
        P("slab", "col", "row", None, None),
        P("slab", "col", "row", None, None, None, None),
        P("slab", "col", "row", None, None),
    )
    return jax.shard_map(
        functools.partial(shards, mesh.shape["slab"]),
        mesh=mesh,
        in_specs=placed,
        out_specs=P("slab", "col", "row", None, None),
        check_vma=False,
    )
```

time: 907 us -> 262 us (0.29)
  waiting for transfers between devices: 604 us -> 0 us
  Pallas kernels: 0 us -> 259 us
  local copies, waits for them, and re-layouts: 127 us -> 3.7 us
  matrix products: 121 us -> 0 us
  starting transfers between devices: 20.7 us -> 0 us
  between operations: 14.3 us -> 0.02 us
  other arithmetic: 11.1 us -> 0 us
    all_gather x8 -> x0, waiting for transfers between devices: 423 us -> none  [shards(): gathered = lax.all_gather(incident, 'col', axis=0, tiled=True)]
    pallas_call x0 -> x1, Pallas kernels: none -> 259 us  [shards(): pl.pallas_call(functools.partial(kernel, (batches, width, blocks, row_blo...]
    gather x12 -> x0, local copies, waits for them, and re-layouts: 127 us -> none  [local_product(): picked = tiles[columns]]
    dot_general x12 -> x0, matrix products: 121 us -> none  [local_product(): jnp.einsum('rkab,rkbw->raw', values, picked, precision=lax.Precision.HIGH...]
    reduce_scatter x12 -> x0, waiting for transfers between devices: 102 us -> none  [the longest x4 44.8 us: shards(): moved = lax.psum_scatter(trans_part, 'row', scatter_dimension=0, tiled=True)]
    ppermute x8 -> x0, waiting for transfers between devices: 78.6 us -> none  [passed_along(): lax.ppermute(value, axis, [(source, source + steps) for source in range(i...]
    ppermute x8 -> x0, starting transfers between devices: 18.7 us -> none  [passed_along(): lax.ppermute(value, axis, [(source, source + steps) for source in range(i...]
  transfers between devices with their start and end apart: 28 -> 0, of which waited for: 25 -> 0; matrix products, arithmetic and copies ran while one was open for 14% -> 0% of each run, Pallas kernels for 0% -> 0%
where the time goes in v1:
time: 262 us
  Pallas kernels  259 us (99%)
  local copies, waits for them, and re-layouts  3.7 us (1%)
    pallas_call x1, Pallas kernels, shards(): pl.pallas_call(functools.partial(kernel, (batches, width, blocks, row_blo...  259 us

profile of v1, /device:TPU:1, one launch (start us, length us, event | category | flops | bytes accessed | tf_op | source)
XLA Modules:
  0.0 262.3 jit_solution(4299424448857297590)
XLA Ops:
  0.0 1.3 copy_bitcast_fusion.1
  1.3 258.6 %shard_map.55 = f32[8,96,128]{2,1,0:T(8,128)} custom-call(f32[384,256]{1,0:T(8,128)} %bitcast.17, f32[6,12,128,128]{3,2,1,0:T(8,128)} %bitcast.13, f32[6,12,128,128]{3,2,1,0:T(8,128)} %bitcast.14, s32[6,12]{1,0:T(8,128)} %get-tuple-element.6.trc_ref, s32[6,12]{1,0:T(8,128)} %get-tuple-element.5.rfc_ref), custom_call_target="tpu_custom_call" | custom-call | tf_op jit(solution)/shard_map/pallas_call | solution.py:310
  259.9 1.3 copy.14
  261.1 0.2 broadcast_in_dim_reshape.3
  261.4 0.9 copy.8

commit v2 on v1

--- a/solution.py
+++ b/solution.py
@@ -9,11 +9,22 @@
 
 MESH = pl.DeviceIdType.MESH
 BATCHES = 8
-STAGE = 5
-TURN = 5
 RING = 4
 PIECES = RING * RING
 BLOCK = 128
+SPREAD = 1
+DONE = 2
+TURN = 2
+GAP = 5
+ROUND = (
+    ("spread", "down", SPREAD),
+    ("spread", "up", SPREAD),
+    ("inject", "down", 0),
+    ("prepare", "", 0),
+    ("finish", "down", DONE),
+    ("inject", "up", 0),
+    ("finish", "up", DONE),
+)
 
 
 def kernel(
@@ -38,7 +49,8 @@
     ex_dst,
     cols,
     load_sem,
-    tree_recv,
+    first_recv,
+    second_recv,
     tree_send,
     ex_recv,
     ex_send,
@@ -78,14 +90,20 @@
             load(op, i).start()
 
     barrier = pltpu.get_barrier_semaphore()
-    greeted = (plane(1, 0), plane(-1, 0), plane(0, 1), plane(0, -1), partner, below, above)
+    near = [plane(d, 0) for d in (1, 2, -1)] + [plane(0, d) for d in (1, 2, -1)]
+    greeted = (*near, partner, below, above)
     for device in greeted:
         pl.semaphore_signal(barrier, inc=1, device_id=device, device_id_type=MESH)
 
+    def place(column):
+        piece = lax.div(column, blocks)
+        turned = lax.rem(piece, RING) * RING + lax.div(piece, RING)
+        return jnp.where(r == 0, piece, turned) * blocks + lax.rem(column, blocks)
+
     for i in range(row_blocks):
         for k in range(picks):
-            cols[0, i, k] = trc_ref[i, k]
-            cols[1, i, k] = rfc_ref[i, k]
+            cols[0, i, k] = place(trc_ref[i, k])
+            cols[1, i, k] = place(rfc_ref[i, k])
     for j in range(blocks):
         turned = jnp.transpose(src_ref[j * BLOCK : (j + 1) * BLOCK, :])
         for n in range(batches):
@@ -93,28 +111,30 @@
 
     pl.semaphore_wait(barrier, len(greeted))
 
-    def tree(n, piece, part, device, group):
-        where = gat.at[n, piece] if part is None else gat.at[n, piece, pl.ds(part * half, half)]
+    mine = b * RING + a
+
+    def tree(where, n, device, arrival):
         pltpu.make_async_remote_copy(
             src_ref=where,
             dst_ref=where,
             send_sem=tree_send.at[n],
-            recv_sem=tree_recv.at[n, group],
+            recv_sem=arrival,
             device_id=device,
             device_id_type=MESH,
         ).start()
 
-    def tree_wait(n, group, count):
+    def arrived(n, count, semaphore):
         some = gat.at[n, pl.ds(0, count)]
-        pltpu.make_async_copy(some, some, tree_recv.at[n, group]).wait()
-
-    def both_sides(n, piece, group):
-        tree(n, piece, None, plane(0, 1), group)
-        tree(n, piece, None, plane(0, -1), group)
-
-    def halves(n, da):
-        tree(n, col(da, -1), 0, plane(0, 1), 5)
-        tree(n, col(da, 1), 1, plane(0, -1), 5)
+        pltpu.make_async_copy(some, some, semaphore).wait()
+
+    def split(n, slot, group):
+        for p in range(RING):
+            at = group * RING + p
+            for j in range(blocks):
+                value = gat[n, at, j * width : (j + 1) * width, :]
+                high = value.astype(jnp.bfloat16)
+                xs[slot, at * blocks + j, 0:width, :] = high
+                xs[slot, at * blocks + j, width : 2 * width, :] = (value - high.astype(jnp.float32)).astype(jnp.bfloat16)
 
     def x_copy(source, n, device):
         return pltpu.make_async_remote_copy(
@@ -126,48 +146,27 @@
             device_id_type=MESH,
         )
 
-    def inject(n, batch, is_down):
-        @pl.when(is_down & (s == 0))
+    def inject(n, batch, slot, is_down):
+        held = src_t if is_down else refl_s
+        end = 0 if is_down else slabs - 1
+
+        @pl.when(s == end)
         def _():
-            gat[n, c] = src_t[batch]
-
-        @pl.when(jnp.logical_not(is_down) & (s == slabs - 1))
-        def _():
-            gat[n, c] = refl_s[batch]
-
-        @pl.when(is_down & (s > 0))
+            gat[n, mine] = held[batch]
+
+        @pl.when(s != end)
         def _():
             x_copy(xrecv.at[n], n, above).wait_recv()
-            gat[n, c] = src_t[batch] + xrecv[n]
-
-        @pl.when(jnp.logical_not(is_down) & (s < slabs - 1))
-        def _():
-            x_copy(xrecv.at[n], n, above).wait_recv()
-            gat[n, c] = refl_s[batch] + xrecv[n]
-
-        tree(n, c, None, plane(1, 0), 0)
-        tree(n, c, None, plane(-1, 0), 0)
-        both_sides(n, c, 2)
-
-    def relay_1(n, batch, is_down):
-        tree_wait(n, 0, 2)
-        tree(n, col(-1, 0), 0, plane(1, 0), 1)
-        tree(n, col(1, 0), 1, plane(-1, 0), 1)
-        both_sides(n, col(-1, 0), 3)
-        both_sides(n, col(1, 0), 3)
-        tree_wait(n, 2, 2)
-        halves(n, 0)
-
-    def relay_2(n, batch, is_down):
-        tree_wait(n, 1, 1)
-        both_sides(n, col(2, 0), 4)
-        tree_wait(n, 3, 4)
-        halves(n, -1)
-        halves(n, 1)
-
-    def relay_3(n, batch, is_down):
-        tree_wait(n, 4, 2)
-        halves(n, 2)
+            gat[n, mine] = held[batch] + xrecv[n]
+
+        for da in (2, 1, -1):
+            tree(gat.at[n, mine], n, plane(da, 0), first_recv.at[n])
+
+    def spread(n, batch, slot, is_down):
+        arrived(n, RING - 1, first_recv.at[n])
+        for order, db in enumerate((2, 1, -1)):
+            tree(gat.at[n, pl.ds(b * RING, RING)], n, plane(0, db), second_recv.at[n, order])
+        split(n, slot, b)
 
     def prepare(item, carry):
         pltpu.make_async_copy(trv_ref.at[0], stage.at[item], load_sem.at[item]).wait()
@@ -189,8 +188,8 @@
             device_id_type=MESH,
         )
 
-    def product(op, i):
-        picked = jnp.concatenate([xs[cols[op, i, k]] for k in range(picks)], axis=1)
+    def product(slot, op, i):
+        picked = jnp.concatenate([xs[slot, cols[op, i, k]] for k in range(picks)], axis=1)
         full = lax.dot_general(
             picked,
             wts[op * row_blocks + i],
@@ -200,40 +199,53 @@
         high, low = full[:width], full[width:]
         return high[:, :BLOCK] + ((high[:, BLOCK:] + low[:, :BLOCK]) + low[:, BLOCK:])
 
-    def apply(n, op):
+    def partner_rows(n, slot, op):
         for j in range(own_rows):
-            ex_src[n, op, j * width : (j + 1) * width, :] = product(op, (1 - r) * own_rows + j)
+            ex_src[n, op, j * width : (j + 1) * width, :] = product(slot, op, (1 - r) * own_rows + j)
         ex_copy(n, op).start()
+
+    def my_rows(n, slot, op):
         for j in range(own_rows):
-            own[op, j * width : (j + 1) * width, :] = product(op, r * own_rows + j)
-
-    def finish(n, batch, is_down):
-        tree_wait(n, 5, RING)
-        for p in range(PIECES):
-            for j in range(blocks):
-                value = gat[n, p, j * width : (j + 1) * width, :]
-                high = value.astype(jnp.bfloat16)
-                xs[p * blocks + j, 0:width, :] = high
-                xs[p * blocks + j, width : 2 * width, :] = (value - high.astype(jnp.float32)).astype(jnp.bfloat16)
-        apply(n, 0)
-
-        @pl.when(is_down)
-        def _():
-            apply(n, 1)
-            ex_copy(n, 0).wait_recv()
-            down_s[batch] = own[0] + ex_dst[n, 0]
+            own[op, j * width : (j + 1) * width, :] = product(slot, op, r * own_rows + j)
+
+    def total(n, op):
+        ex_copy(n, op).wait_recv()
+        return own[op] + ex_dst[n, op]
+
+    def finish(n, batch, slot, is_down):
+        for order, db in ((1, 1), (2, -1), (0, 2)):
+            arrived(n, RING, second_recv.at[n, order])
+            split(n, slot, lax.rem(b - db + RING, RING))
+        if is_down:
+            first = lax.div(s, slabs - 1)
+            second = 1 - first
+            partner_rows(n, slot, first)
+            my_rows(n, slot, first)
+            partner_rows(n, slot, second)
 
             @pl.when(s < slabs - 1)
             def _():
+                down_s[batch] = total(n, 0)
                 x_copy(down_s.at[batch], n, below).start()
 
-            ex_copy(n, 1).wait_recv()
-            refl_s[batch] = own[1] + ex_dst[n, 1]
-
-        @pl.when(jnp.logical_not(is_down))
-        def _():
-            ex_copy(n, 0).wait_recv()
-            up_s[batch] = own[0] + ex_dst[n, 0]
+            @pl.when(s == slabs - 1)
+            def _():
+                refl_s[batch] = total(n, 1)
+
+            my_rows(n, slot, second)
+
+            @pl.when(s < slabs - 1)
+            def _():
+                refl_s[batch] = total(n, 1)
+
+            @pl.when(s == slabs - 1)
+            def _():
+                down_s[batch] = total(n, 0)
+
+        else:
+            partner_rows(n, slot, 0)
+            my_rows(n, slot, 0)
+            up_s[batch] = total(n, 0)
 
             @pl.when(s > 0)
             def _():
@@ -241,39 +253,36 @@
 
             out_ref[batch] = down_s[batch] + up_s[batch]
 
-    offset = (2 * (slabs - 1) - 2 * s) * STAGE + TURN
-
-    def phase(body, slot, delay, first=0):
-        at = slot - delay + 2 * batches
-        is_down = lax.rem(at, 2) == 0
-        batch = jnp.where(is_down, lax.div(at, 2) - batches, lax.div(at - offset + 64, 2) - batches - 32)
-        valid = (batch >= 0) & (batch < batches)
-
-        @pl.when(valid)
-        def _():
-            body(jnp.where(is_down, batch, batches + batch), batch, is_down)
-
+    offset = TURN + (slabs - 1 - s) * GAP
+    bodies = {"inject": inject, "spread": spread, "finish": finish}
+    keep = DONE - SPREAD + 1
     items = 2 * row_blocks
-    each = 3
+    each = items // DONE
 
     @pl.when(s > 0)
     def _():
         lax.fori_loop(0, items, prepare, 0)
 
-    def slot_body(slot, carry):
-        phase(relay_3, slot, 3)
-        phase(relay_2, slot, 2)
-        phase(relay_1, slot, 1)
-        phase(inject, slot, 0)
-
-        @pl.when((s == 0) & (slot < items // each))
-        def _():
-            lax.fori_loop(slot * each, slot * each + each, prepare, 0)
-
-        phase(finish, slot, 4)
+    def round_body(step, carry):
+        for kind, way, delay in ROUND:
+            if kind == "prepare":
+
+                @pl.when((s == 0) & (step < DONE))
+                def _():
+                    lax.fori_loop(step * each, step * each + each, prepare, 0)
+
+                continue
+            is_down = way == "down"
+            batch = step - delay - (0 if is_down else offset)
+
+            @pl.when((batch >= 0) & (batch < batches))
+            def _():
+                slot = lax.rem(batch, keep) + (0 if is_down else keep)
+                bodies[kind](batch + (0 if is_down else batches), batch, slot, is_down)
+
         return carry
 
-    lax.fori_loop(0, 2 * (batches - 1) + offset + 5, slot_body, 0)
+    lax.fori_loop(0, batches + offset + DONE, round_body, 0)
 
     def drain(n, carry):
         sent = gat.at[n, pl.ds(0, PIECES - 1)]
@@ -314,7 +323,7 @@
         out_specs=vmem,
         scratch_shapes=[
             pltpu.VMEM((tasks, PIECES, rows, BLOCK), f32),
-            pltpu.VMEM((PIECES * blocks, 2 * width, BLOCK), bf16),
+            pltpu.VMEM((2 * (DONE - SPREAD + 1), PIECES * blocks, 2 * width, BLOCK), bf16),
             pltpu.VMEM((2 * row_blocks, 2 * BLOCK, picks * BLOCK), bf16),
             pltpu.VMEM((2 * row_blocks, picks, BLOCK, BLOCK), f32),
             pltpu.VMEM((batches, rows, BLOCK), f32),
@@ -327,7 +336,8 @@
             pltpu.VMEM((tasks, 2, rows, BLOCK), f32),
             pltpu.SMEM((2, row_blocks, picks), jnp.int32),
             dma((2 * row_blocks,)),
-            dma((tasks, 6)),
+            dma((tasks,)),
+            dma((tasks, RING - 1)),
             dma((tasks,)),
             dma((tasks, 2)),
             dma((tasks, 2)),

time: 262 us -> 221 us (0.84)
  Pallas kernels: 259 us -> 218 us
    pallas_call x1, Pallas kernels: 259 us -> 218 us  [shards(): pl.pallas_call(functools.partial(kernel, (batches, width, blocks, row_blo...]
where the time goes in v2:
time: 221 us
  Pallas kernels  218 us (99%)
  local copies, waits for them, and re-layouts  3.7 us (2%)
    pallas_call x1, Pallas kernels, shards(): pl.pallas_call(functools.partial(kernel, (batches, width, blocks, row_blo...  218 us

profile of v2, /device:TPU:1, one launch (start us, length us, event | category | flops | bytes accessed | tf_op | source)
XLA Modules:
  0.0 221.3 jit_solution(10214694478259925351)
XLA Ops:
  0.0 1.3 copy_bitcast_fusion.1
  1.3 217.5 %shard_map.55 = f32[8,96,128]{2,1,0:T(8,128)} custom-call(f32[384,256]{1,0:T(8,128)} %bitcast.17, f32[6,12,128,128]{3,2,1,0:T(8,128)} %bitcast.13, f32[6,12,128,128]{3,2,1,0:T(8,128)} %bitcast.14, s32[6,12]{1,0:T(8,128)} %get-tuple-element.6.trc_ref, s32[6,12]{1,0:T(8,128)} %get-tuple-element.5.rfc_ref), custom_call_target="tpu_custom_call" | custom-call | tf_op jit(solution)/shard_map/pallas_call | solution.py:319
  218.8 1.3 copy.14
  220.1 0.2 broadcast_in_dim_reshape.3
  220.3 0.9 copy.8

commit v3 on v2

--- a/solution.py
+++ b/solution.py
@@ -40,6 +40,7 @@
     wts,
     stage,
     src_t,
+    out_t,
     xrecv,
     down_s,
     refl_s,
@@ -58,8 +59,6 @@
     x_send,
 ):
     batches, width, blocks, row_blocks, picks, slabs = dims
-    rows = blocks * width
-    half = rows // 2
     own_rows = row_blocks // 2
     s = lax.axis_index("slab")
     r = lax.axis_index("row")
@@ -95,15 +94,6 @@
     for device in greeted:
         pl.semaphore_signal(barrier, inc=1, device_id=device, device_id_type=MESH)
 
-    def place(column):
-        piece = lax.div(column, blocks)
-        turned = lax.rem(piece, RING) * RING + lax.div(piece, RING)
-        return jnp.where(r == 0, piece, turned) * blocks + lax.rem(column, blocks)
-
-    for i in range(row_blocks):
-        for k in range(picks):
-            cols[0, i, k] = place(trc_ref[i, k])
-            cols[1, i, k] = place(rfc_ref[i, k])
     for j in range(blocks):
         turned = jnp.transpose(src_ref[j * BLOCK : (j + 1) * BLOCK, :])
         for n in range(batches):
@@ -111,12 +101,12 @@
 
     pl.semaphore_wait(barrier, len(greeted))
 
-    mine = b * RING + a
-
-    def tree(where, n, device, arrival):
+    mine = b * RING
+
+    def tree(source, target, n, device, arrival):
         pltpu.make_async_remote_copy(
-            src_ref=where,
-            dst_ref=where,
+            src_ref=source,
+            dst_ref=target,
             send_sem=tree_send.at[n],
             recv_sem=arrival,
             device_id=device,
@@ -130,11 +120,12 @@
     def split(n, slot, group):
         for p in range(RING):
             at = group * RING + p
+            to = (lax.rem(a + p, RING) * step_a + group * step_b) * blocks
             for j in range(blocks):
                 value = gat[n, at, j * width : (j + 1) * width, :]
                 high = value.astype(jnp.bfloat16)
-                xs[slot, at * blocks + j, 0:width, :] = high
-                xs[slot, at * blocks + j, width : 2 * width, :] = (value - high.astype(jnp.float32)).astype(jnp.bfloat16)
+                xs[slot, to + j, 0:width, :] = high
+                xs[slot, to + j, width : 2 * width, :] = (value - high.astype(jnp.float32)).astype(jnp.bfloat16)
 
     def x_copy(source, n, device):
         return pltpu.make_async_remote_copy(
@@ -159,30 +150,34 @@
             x_copy(xrecv.at[n], n, above).wait_recv()
             gat[n, mine] = held[batch] + xrecv[n]
 
+        own_piece = gat.at[n, mine]
         for da in (2, 1, -1):
-            tree(gat.at[n, mine], n, plane(da, 0), first_recv.at[n])
+            tree(own_piece, gat.at[n, mine + (RING - da) % RING], n, plane(da, 0), first_recv.at[n])
+        for order, db in enumerate((2, 1, -1)):
+            tree(own_piece, own_piece, n, plane(0, db), second_recv.at[n, order])
 
     def spread(n, batch, slot, is_down):
         arrived(n, RING - 1, first_recv.at[n])
+        others = gat.at[n, pl.ds(mine + 1, RING - 1)]
         for order, db in enumerate((2, 1, -1)):
-            tree(gat.at[n, pl.ds(b * RING, RING)], n, plane(0, db), second_recv.at[n, order])
+            tree(others, others, n, plane(0, db), second_recv.at[n, order])
         split(n, slot, b)
 
     def prepare(item, carry):
         pltpu.make_async_copy(trv_ref.at[0], stage.at[item], load_sem.at[item]).wait()
         for k in range(picks):
-            value = stage[item, k]
+            value = jnp.transpose(stage[item, k])
             high = value.astype(jnp.bfloat16)
             low = (value - high.astype(jnp.float32)).astype(jnp.bfloat16)
-            wts[item, 0:BLOCK, k * BLOCK : (k + 1) * BLOCK] = high
-            wts[item, BLOCK : 2 * BLOCK, k * BLOCK : (k + 1) * BLOCK] = low
+            wts[item, k * BLOCK : (k + 1) * BLOCK, 0:BLOCK] = high
+            wts[item, k * BLOCK : (k + 1) * BLOCK, BLOCK : 2 * BLOCK] = low
         return carry
 
     def ex_copy(n, op):
         return pltpu.make_async_remote_copy(
             src_ref=ex_src.at[n, op],
             dst_ref=ex_dst.at[n, op],
-            send_sem=ex_send.at[n, op],
+            send_sem=ex_send.at[n],
             recv_sem=ex_recv.at[n, op],
             device_id=partner,
             device_id_type=MESH,
@@ -193,7 +188,7 @@
         full = lax.dot_general(
             picked,
             wts[op * row_blocks + i],
-            (((1,), (1,)), ((), ())),
+            (((1,), (0,)), ((), ())),
             preferred_element_type=jnp.float32,
         )
         high, low = full[:width], full[width:]
@@ -204,7 +199,7 @@
             ex_src[n, op, j * width : (j + 1) * width, :] = product(slot, op, (1 - r) * own_rows + j)
         ex_copy(n, op).start()
 
-    def my_rows(n, slot, op):
+    def my_rows(slot, op):
         for j in range(own_rows):
             own[op, j * width : (j + 1) * width, :] = product(slot, op, r * own_rows + j)
 
@@ -220,7 +215,7 @@
             first = lax.div(s, slabs - 1)
             second = 1 - first
             partner_rows(n, slot, first)
-            my_rows(n, slot, first)
+            my_rows(slot, first)
             partner_rows(n, slot, second)
 
             @pl.when(s < slabs - 1)
@@ -232,7 +227,7 @@
             def _():
                 refl_s[batch] = total(n, 1)
 
-            my_rows(n, slot, second)
+            my_rows(slot, second)
 
             @pl.when(s < slabs - 1)
             def _():
@@ -244,14 +239,17 @@
 
         else:
             partner_rows(n, slot, 0)
-            my_rows(n, slot, 0)
+            my_rows(slot, 0)
             up_s[batch] = total(n, 0)
 
             @pl.when(s > 0)
             def _():
                 x_copy(up_s.at[batch], n, above).start()
 
-            out_ref[batch] = down_s[batch] + up_s[batch]
+            start = pl.ds(pl.multiple_of(batch * width, width), width)
+            for j in range(blocks):
+                at = pl.ds(j * width, width)
+                out_t[j, start, :] = down_s[batch, at, :] + up_s[batch, at, :]
 
     offset = TURN + (slabs - 1 - s) * GAP
     bodies = {"inject": inject, "spread": spread, "finish": finish}
@@ -259,6 +257,12 @@
     items = 2 * row_blocks
     each = items // DONE
 
+    def tables():
+        for i in range(row_blocks):
+            for k in range(picks):
+                cols[0, i, k] = trc_ref[i, 0, k]
+                cols[1, i, k] = rfc_ref[i, 0, k]
+
     @pl.when(s > 0)
     def _():
         lax.fori_loop(0, items, prepare, 0)
@@ -267,6 +271,8 @@
         for kind, way, delay in ROUND:
             if kind == "prepare":
 
+                pl.when(step == 0)(tables)
+
                 @pl.when((s == 0) & (step < DONE))
                 def _():
                     lax.fori_loop(step * each, step * each + each, prepare, 0)
@@ -284,16 +290,23 @@
 
     lax.fori_loop(0, batches + offset + DONE, round_body, 0)
 
+    for j in range(blocks):
+        out_ref[j * BLOCK : (j + 1) * BLOCK, :] = jnp.transpose(out_t[j])
+
     def drain(n, carry):
+        is_down = n < batches
         sent = gat.at[n, pl.ds(0, PIECES - 1)]
         pltpu.make_async_copy(sent, sent, tree_send.at[n]).wait()
-        ex_copy(n, 0).wait_send()
-
-        @pl.when(n < batches)
-        def _():
-            ex_copy(n, 1).wait_send()
-
-        @pl.when(((n < batches) & (s < slabs - 1)) | ((n >= batches) & (s > 0)))
+
+        @pl.when(is_down)
+        def _():
+            pltpu.make_async_copy(ex_src.at[n], ex_src.at[n], ex_send.at[n]).wait()
+
+        @pl.when(jnp.logical_not(is_down))
+        def _():
+            ex_copy(n, 0).wait_send()
+
+        @pl.when((is_down & (s < slabs - 1)) | (jnp.logical_not(is_down) & (s > 0)))
         def _():
             x_copy(up_s.at[0], n, above).wait_send()
 
@@ -318,15 +331,16 @@
     dma = pltpu.SemaphoreType.DMA
     out = pl.pallas_call(
         functools.partial(kernel, (batches, width, blocks, row_blocks, picks, slabs)),
-        out_shape=jax.ShapeDtypeStruct((batches, rows, BLOCK), f32),
+        out_shape=jax.ShapeDtypeStruct((rows_in, span), f32),
         in_specs=[vmem, hbm, hbm, smem, smem],
         out_specs=vmem,
         scratch_shapes=[
             pltpu.VMEM((tasks, PIECES, rows, BLOCK), f32),
             pltpu.VMEM((2 * (DONE - SPREAD + 1), PIECES * blocks, 2 * width, BLOCK), bf16),
-            pltpu.VMEM((2 * row_blocks, 2 * BLOCK, picks * BLOCK), bf16),
+            pltpu.VMEM((2 * row_blocks, picks * BLOCK, 2 * BLOCK), bf16),
             pltpu.VMEM((2 * row_blocks, picks, BLOCK, BLOCK), f32),
             pltpu.VMEM((batches, rows, BLOCK), f32),
+            pltpu.VMEM((blocks, span, BLOCK), f32),
             pltpu.VMEM((tasks, rows, BLOCK), f32),
             pltpu.VMEM((batches, rows, BLOCK), f32),
             pltpu.VMEM((batches, rows, BLOCK), f32),
@@ -340,7 +354,7 @@
             dma((tasks, RING - 1)),
             dma((tasks,)),
             dma((tasks, 2)),
-            dma((tasks, 2)),
+            dma((tasks,)),
             dma((tasks,)),
             dma((tasks,)),
         ],
@@ -349,9 +363,8 @@
             has_side_effects=True,
             vmem_limit_bytes=60 * 1024 * 1024,
         ),
-    )(source, tr_vals[0, 0, 0], rf_vals[0, 0, 0], tr_cols[0, 0, 0], rf_cols[0, 0, 0])
-    out = out.reshape(batches, blocks, width, BLOCK).transpose(1, 3, 0, 2)
-    return out.reshape(rows_in, span)[None, None, None]
+    )(source, tr_vals[0, 0, 0], rf_vals[0, 0, 0], tr_cols[0, 0, 0][:, None], rf_cols[0, 0, 0][:, None])
+    return out[None, None, None]
 
 
 def solution(mesh):

time: 221 us -> 205 us (0.928)
  Pallas kernels: 218 us -> 203 us
    pallas_call x1, Pallas kernels: 218 us -> 203 us  [shards(): pl.pallas_call(functools.partial(kernel, (batches, width, blocks, row_blo...]
where the time goes in v3:
time: 205 us
  Pallas kernels  203 us (99%)
    pallas_call x1, Pallas kernels, shards(): pl.pallas_call(functools.partial(kernel, (batches, width, blocks, row_blo...  203 us

profile of v3, /device:TPU:1, one launch (start us, length us, event | category | flops | bytes accessed | tf_op | source)
XLA Modules:
  0.0 204.6 jit_solution(828948149397573926)
XLA Ops:
  0.0 202.8 %shard_map.55 = f32[384,256]{1,0:T(8,128)} custom-call(f32[384,256]{1,0:T(8,128)} %bitcast.9, f32[6,12,128,128]{3,2,1,0:T(8,128)} %bitcast.6, f32[6,12,128,128]{3,2,1,0:T(8,128)} %bitcast.7, s32[6,1,12]{2,1,0:T(1,128)} %bitcast.10, s32[6,1,12]{2,1,0:T(1,128)} %bitcast.11), custom_call_target="tpu_custom_call" | custom-call | tf_op jit(solution)/shard_map/pallas_call | solution.py:332
  202.8 1.8 copy.7

commit v4 on v3

--- a/solution.py
+++ b/solution.py
@@ -8,22 +8,29 @@
 from jax.sharding import PartitionSpec as P
 
 MESH = pl.DeviceIdType.MESH
-BATCHES = 8
+BATCHES = 16
 RING = 4
 PIECES = RING * RING
 BLOCK = 128
-SPREAD = 1
-DONE = 2
-TURN = 2
-GAP = 5
-ROUND = (
-    ("spread", "down", SPREAD),
-    ("spread", "up", SPREAD),
+RELAYED = False
+TURN = 4
+GAP = 8
+KEEP = 3
+OTHERS = (
     ("inject", "down", 0),
-    ("prepare", "", 0),
-    ("finish", "down", DONE),
+    ("spread", "down", 1),
     ("inject", "up", 0),
-    ("finish", "up", DONE),
+    ("spread", "up", 1),
+    ("finish", "up", 3),
+    ("finish", "down", 2),
+)
+LAST = (
+    ("inject", "up", 0),
+    ("finish", "down", 3),
+    ("inject", "down", 0),
+    ("spread", "down", 1),
+    ("spread", "up", 1),
+    ("finish", "up", 3),
 )
 
 
@@ -127,6 +134,14 @@
                 xs[slot, to + j, 0:width, :] = high
                 xs[slot, to + j, width : 2 * width, :] = (value - high.astype(jnp.float32)).astype(jnp.bfloat16)
 
+    def to_second(pieces, n):
+        @pl.when((s < slabs - 1) | (not RELAYED))
+        def _():
+            tree(pieces, pieces, n, plane(0, 2), second_recv.at[n, 0])
+
+        for order, db in ((1, 1), (2, -1)):
+            tree(pieces, pieces, n, plane(0, db), second_recv.at[n, order])
+
     def x_copy(source, n, device):
         return pltpu.make_async_remote_copy(
             src_ref=source,
@@ -153,15 +168,24 @@
         own_piece = gat.at[n, mine]
         for da in (2, 1, -1):
             tree(own_piece, gat.at[n, mine + (RING - da) % RING], n, plane(da, 0), first_recv.at[n])
-        for order, db in enumerate((2, 1, -1)):
-            tree(own_piece, own_piece, n, plane(0, db), second_recv.at[n, order])
+        to_second(own_piece, n)
 
     def spread(n, batch, slot, is_down):
         arrived(n, RING - 1, first_recv.at[n])
         others = gat.at[n, pl.ds(mine + 1, RING - 1)]
-        for order, db in enumerate((2, 1, -1)):
-            tree(others, others, n, plane(0, db), second_recv.at[n, order])
+        to_second(others, n)
         split(n, slot, b)
+
+    def relay(n, batch, slot, is_down):
+        @pl.when(s == slabs - 1)
+        def _():
+            for order, db in ((1, 1), (2, -1)):
+                arrived(n, RING, second_recv.at[n, order])
+                group = lax.rem(b - db + RING, RING)
+                passed = gat.at[n, pl.ds(group * RING + (order - 1) * RING // 2, RING // 2)]
+                tree(passed, passed, n, plane(0, db), second_recv.at[n, 0])
+            for db in (1, -1):
+                split(n, slot, lax.rem(b - db + RING, RING))
 
     def prepare(item, carry):
         pltpu.make_async_copy(trv_ref.at[0], stage.at[item], load_sem.at[item]).wait()
@@ -208,9 +232,14 @@
         return own[op] + ex_dst[n, op]
 
     def finish(n, batch, slot, is_down):
-        for order, db in ((1, 1), (2, -1), (0, 2)):
-            arrived(n, RING, second_recv.at[n, order])
-            split(n, slot, lax.rem(b - db + RING, RING))
+        @pl.when((s < slabs - 1) | (not RELAYED))
+        def _():
+            for order, db in ((1, 1), (2, -1)):
+                arrived(n, RING, second_recv.at[n, order])
+                split(n, slot, lax.rem(b - db + RING, RING))
+
+        arrived(n, RING, second_recv.at[n, 0])
+        split(n, slot, lax.rem(b + 2, RING))
         if is_down:
             first = lax.div(s, slabs - 1)
             second = 1 - first
@@ -252,10 +281,10 @@
                 out_t[j, start, :] = down_s[batch, at, :] + up_s[batch, at, :]
 
     offset = TURN + (slabs - 1 - s) * GAP
-    bodies = {"inject": inject, "spread": spread, "finish": finish}
-    keep = DONE - SPREAD + 1
+    bodies = {"inject": inject, "spread": spread, "relay": relay, "finish": finish}
     items = 2 * row_blocks
-    each = items // DONE
+    each = items // 2
+    longest = max(delay for _, _, delay in OTHERS + LAST)
 
     def tables():
         for i in range(row_blocks):
@@ -265,30 +294,31 @@
 
     @pl.when(s > 0)
     def _():
+        tables()
         lax.fori_loop(0, items, prepare, 0)
 
-    def round_body(step, carry):
-        for kind, way, delay in ROUND:
-            if kind == "prepare":
-
-                pl.when(step == 0)(tables)
-
-                @pl.when((s == 0) & (step < DONE))
-                def _():
-                    lax.fori_loop(step * each, step * each + each, prepare, 0)
-
-                continue
+    def round_body(order, step, carry):
+        for kind, way, delay in order:
             is_down = way == "down"
             batch = step - delay - (0 if is_down else offset)
 
             @pl.when((batch >= 0) & (batch < batches))
             def _():
-                slot = lax.rem(batch, keep) + (0 if is_down else keep)
+                slot = lax.rem(batch, KEEP) + (0 if is_down else KEEP)
                 bodies[kind](batch + (0 if is_down else batches), batch, slot, is_down)
 
+        @pl.when((s == 0) & (step < 2))
+        def _():
+            pl.when(step == 0)(tables)
+            lax.fori_loop(step * each, step * each + each, prepare, 0)
+
         return carry
 
-    lax.fori_loop(0, batches + offset + DONE, round_body, 0)
+    for order, here in ((OTHERS, s < slabs - 1), (LAST, s == slabs - 1)):
+
+        @pl.when(here)
+        def _():
+            lax.fori_loop(0, batches + offset + longest, functools.partial(round_body, order), 0)
 
     for j in range(blocks):
         out_ref[j * BLOCK : (j + 1) * BLOCK, :] = jnp.transpose(out_t[j])
@@ -336,7 +366,7 @@
         out_specs=vmem,
         scratch_shapes=[
             pltpu.VMEM((tasks, PIECES, rows, BLOCK), f32),
-            pltpu.VMEM((2 * (DONE - SPREAD + 1), PIECES * blocks, 2 * width, BLOCK), bf16),
+            pltpu.VMEM((2 * KEEP, PIECES * blocks, 2 * width, BLOCK), bf16),
             pltpu.VMEM((2 * row_blocks, picks * BLOCK, 2 * BLOCK), bf16),
             pltpu.VMEM((2 * row_blocks, picks, BLOCK, BLOCK), f32),
             pltpu.VMEM((batches, rows, BLOCK), f32),

time: 205 us -> 196 us (0.956)
  Pallas kernels: 203 us -> 194 us
    pallas_call x1, Pallas kernels: 203 us -> 194 us  [shards(): pl.pallas_call(functools.partial(kernel, (batches, width, blocks, row_blo...]
where the time goes in v4:
time: 196 us
  Pallas kernels  194 us (99%)
    pallas_call x1, Pallas kernels, shards(): pl.pallas_call(functools.partial(kernel, (batches, width, blocks, row_blo...  194 us

profile of v4, /device:TPU:1, one launch (start us, length us, event | category | flops | bytes accessed | tf_op | source)
XLA Modules:
  0.0 195.6 jit_solution(3597693121388022255)
XLA Ops:
  0.0 193.8 %shard_map.55 = f32[384,256]{1,0:T(8,128)} custom-call(f32[384,256]{1,0:T(8,128)} %bitcast.9, f32[6,12,128,128]{3,2,1,0:T(8,128)} %bitcast.6, f32[6,12,128,128]{3,2,1,0:T(8,128)} %bitcast.7, s32[6,1,12]{2,1,0:T(1,128)} %bitcast.10, s32[6,1,12]{2,1,0:T(1,128)} %bitcast.11), custom_call_target="tpu_custom_call" | custom-call | tf_op jit(solution)/shard_map/pallas_call | solution.py:362
  193.8 1.8 copy.7

commit v5 on v4

--- a/solution.py
+++ b/solution.py
@@ -12,16 +12,17 @@
 RING = 4
 PIECES = RING * RING
 BLOCK = 128
-RELAYED = False
 TURN = 4
 GAP = 8
 KEEP = 3
 OTHERS = (
     ("inject", "down", 0),
     ("spread", "down", 1),
+    ("settle", "down", 3),
     ("inject", "up", 0),
     ("spread", "up", 1),
     ("finish", "up", 3),
+    ("settle", "up", 3),
     ("finish", "down", 2),
 )
 LAST = (
@@ -29,8 +30,10 @@
     ("finish", "down", 3),
     ("inject", "down", 0),
     ("spread", "down", 1),
+    ("settle", "down", 3),
     ("spread", "up", 1),
     ("finish", "up", 3),
+    ("settle", "up", 3),
 )
 
 
@@ -135,11 +138,45 @@
                 xs[slot, to + j, width : 2 * width, :] = (value - high.astype(jnp.float32)).astype(jnp.bfloat16)
 
     def to_second(pieces, n):
-        @pl.when((s < slabs - 1) | (not RELAYED))
-        def _():
-            tree(pieces, pieces, n, plane(0, 2), second_recv.at[n, 0])
-
-        for order, db in ((1, 1), (2, -1)):
+        for order, db in ((1, 1), (2, -1), (0, 2)):
+            tree(pieces, pieces, n, plane(0, db), second_recv.at[n, order])
+
+    def x_copy(source, n, device):
+        return pltpu.make_async_remote_copy(
+            src_ref=source,
+            dst_ref=xrecv.at[n],
+            send_sem=x_send.at[n],
+            recv_sem=x_recv.at[n],
+            device_id=device,
+            device_id_type=MESH,
+        )
+
+    def inject(n, batch, slot, is_down):
+        held = src_t if is_down else refl_s
+        end = 0 if is_down else slabs - 1
+
+        @pl.when(s == end)
+        def _():
+            gat[n, mine] = held[batch]
+
+        @pl.when(s != end)
+        def _():
+            x_copy(xrecv.at[n], n, above).wait_recv()
+            gat[n, mine] = held[batch] + xrecv[n]
+
+        own_piece = gat.at[n, mine]
+        for da in (2, 1, -1):
+            tree(own_piece, gat.at[n, mine + (RING - da) % RING], n, plane(da, 0), first_recv.at[n])
+        to_second(own_piece, n)
+
+    def spread(n, batch, slot, is_down):
+        arrived(n, RING - 1, first_recv.at[n])
+        others = gat.at[n, pl.ds(mine + 1, RING - 1)]
+        to_second(others, n)
+        split(n, slot, b)
+
+    def to_second(pieces, n):
+        for order, db in ((1, 1), (2, -1), (0, 2)):
             tree(pieces, pieces, n, plane(0, db), second_recv.at[n, order])
 
     def x_copy(source, n, device):
@@ -223,53 +260,53 @@
             ex_src[n, op, j * width : (j + 1) * width, :] = product(slot, op, (1 - r) * own_rows + j)
         ex_copy(n, op).start()
 
-    def my_rows(slot, op):
+    def my_rows(slot, op, keep):
         for j in range(own_rows):
-            own[op, j * width : (j + 1) * width, :] = product(slot, op, r * own_rows + j)
-
-    def total(n, op):
+            own[keep, j * width : (j + 1) * width, :] = product(slot, op, r * own_rows + j)
+
+    def total(n, op, kept):
         ex_copy(n, op).wait_recv()
-        return own[op] + ex_dst[n, op]
+        return own[kept] + ex_dst[n, op]
 
     def finish(n, batch, slot, is_down):
-        @pl.when((s < slabs - 1) | (not RELAYED))
-        def _():
-            for order, db in ((1, 1), (2, -1)):
-                arrived(n, RING, second_recv.at[n, order])
-                split(n, slot, lax.rem(b - db + RING, RING))
-
-        arrived(n, RING, second_recv.at[n, 0])
-        split(n, slot, lax.rem(b + 2, RING))
+        for order, db in ((1, 1), (2, -1), (0, 2)):
+            arrived(n, RING, second_recv.at[n, order])
+            split(n, slot, lax.rem(b - db + RING, RING))
+
         if is_down:
             first = lax.div(s, slabs - 1)
             second = 1 - first
             partner_rows(n, slot, first)
-            my_rows(slot, first)
+            my_rows(slot, first, 0)
             partner_rows(n, slot, second)
 
             @pl.when(s < slabs - 1)
             def _():
-                down_s[batch] = total(n, 0)
+                down_s[batch] = total(n, 0, 0)
                 x_copy(down_s.at[batch], n, below).start()
 
             @pl.when(s == slabs - 1)
             def _():
-                refl_s[batch] = total(n, 1)
-
-            my_rows(slot, second)
-
-            @pl.when(s < slabs - 1)
-            def _():
-                refl_s[batch] = total(n, 1)
-
-            @pl.when(s == slabs - 1)
-            def _():
-                down_s[batch] = total(n, 0)
-
+                refl_s[batch] = total(n, 1, 0)
+
+            my_rows(slot, second, 1)
         else:
             partner_rows(n, slot, 0)
-            my_rows(slot, 0)
-            up_s[batch] = total(n, 0)
+            my_rows(slot, 0, 2)
+
+    def settle(n, batch, slot, is_down):
+        if is_down:
+
+            @pl.when(s < slabs - 1)
+            def _():
+                refl_s[batch] = total(n, 1, 1)
+
+            @pl.when(s == slabs - 1)
+            def _():
+                down_s[batch] = total(n, 0, 1)
+
+        else:
+            up_s[batch] = total(n, 0, 2)
 
             @pl.when(s > 0)
             def _():
@@ -281,7 +318,7 @@
                 out_t[j, start, :] = down_s[batch, at, :] + up_s[batch, at, :]
 
     offset = TURN + (slabs - 1 - s) * GAP
-    bodies = {"inject": inject, "spread": spread, "relay": relay, "finish": finish}
+    bodies = {"inject": inject, "spread": spread, "finish": finish, "settle": settle}
     items = 2 * row_blocks
     each = items // 2
     longest = max(delay for _, _, delay in OTHERS + LAST)
@@ -375,7 +412,7 @@
             pltpu.VMEM((batches, rows, BLOCK), f32),
             pltpu.VMEM((batches, rows, BLOCK), f32),
             pltpu.VMEM((batches, rows, BLOCK), f32),
-            pltpu.VMEM((2, rows, BLOCK), f32),
+            pltpu.VMEM((3, rows, BLOCK), f32),
             pltpu.VMEM((tasks, 2, rows, BLOCK), f32),
             pltpu.VMEM((tasks, 2, rows, BLOCK), f32),
             pltpu.SMEM((2, row_blocks, picks), jnp.int32),

time: 196 us -> 194 us (0.990)
  Pallas kernels: 194 us -> 192 us
where the time goes in v5:
time: 194 us
  Pallas kernels  192 us (99%)
    pallas_call x1, Pallas kernels, shards(): pl.pallas_call(functools.partial(kernel, (batches, width, blocks, row_blo...  192 us

profile of v5, /device:TPU:1, one launch (start us, length us, event | category | flops | bytes accessed | tf_op | source)
XLA Modules:
  0.0 194.0 jit_solution(2441466452105306081)
XLA Ops:
  0.0 192.2 %shard_map.55 = f32[384,256]{1,0:T(8,128)} custom-call(f32[384,256]{1,0:T(8,128)} %bitcast.9, f32[6,12,128,128]{3,2,1,0:T(8,128)} %bitcast.6, f32[6,12,128,128]{3,2,1,0:T(8,128)} %bitcast.7, s32[6,1,12]{2,1,0:T(1,128)} %bitcast.10, s32[6,1,12]{2,1,0:T(1,128)} %bitcast.11), custom_call_target="tpu_custom_call" | custom-call | tf_op jit(solution)/shard_map/pallas_call | solution.py:399
  192.3 1.8 copy.7

commit v6 on v5

--- a/solution.py
+++ b/solution.py
@@ -117,7 +117,7 @@
         pltpu.make_async_remote_copy(
             src_ref=source,
             dst_ref=target,
-            send_sem=tree_send.at[n],
+            send_sem=tree_send.at[lax.div(n, batches)],
             recv_sem=arrival,
             device_id=device,
             device_id_type=MESH,
@@ -145,7 +145,7 @@
         return pltpu.make_async_remote_copy(
             src_ref=source,
             dst_ref=xrecv.at[n],
-            send_sem=x_send.at[n],
+            send_sem=x_send,
             recv_sem=x_recv.at[n],
             device_id=device,
             device_id_type=MESH,
@@ -183,7 +183,7 @@
         return pltpu.make_async_remote_copy(
             src_ref=source,
             dst_ref=xrecv.at[n],
-            send_sem=x_send.at[n],
+            send_sem=x_send,
             recv_sem=x_recv.at[n],
             device_id=device,
             device_id_type=MESH,
@@ -238,7 +238,7 @@
         return pltpu.make_async_remote_copy(
             src_ref=ex_src.at[n, op],
             dst_ref=ex_dst.at[n, op],
-            send_sem=ex_send.at[n],
+            send_sem=ex_send,
             recv_sem=ex_recv.at[n, op],
             device_id=partner,
             device_id_type=MESH,
@@ -360,26 +360,20 @@
     for j in range(blocks):
         out_ref[j * BLOCK : (j + 1) * BLOCK, :] = jnp.transpose(out_t[j])
 
-    def drain(n, carry):
-        is_down = n < batches
-        sent = gat.at[n, pl.ds(0, PIECES - 1)]
-        pltpu.make_async_copy(sent, sent, tree_send.at[n]).wait()
-
-        @pl.when(is_down)
-        def _():
-            pltpu.make_async_copy(ex_src.at[n], ex_src.at[n], ex_send.at[n]).wait()
-
-        @pl.when(jnp.logical_not(is_down))
-        def _():
-            ex_copy(n, 0).wait_send()
-
-        @pl.when((is_down & (s < slabs - 1)) | (jnp.logical_not(is_down) & (s > 0)))
-        def _():
-            x_copy(up_s.at[0], n, above).wait_send()
-
-        return carry
-
-    lax.fori_loop(0, 2 * batches, drain, 0)
+    def drained(sent, semaphore):
+        pltpu.make_async_copy(sent, sent, semaphore).wait()
+
+    for way in range(2):
+        drained(gat.at[pl.ds(0, batches), pl.ds(0, PIECES - 1)], tree_send.at[way])
+    drained(ex_src.at[pl.ds(0, 3 * batches // 2)], ex_send)
+
+    @pl.when((s > 0) & (s < slabs - 1))
+    def _():
+        drained(xrecv, x_send)
+
+    @pl.when((s == 0) | (s == slabs - 1))
+    def _():
+        drained(xrecv.at[pl.ds(0, batches)], x_send)
 
 
 def shards(slabs, sources, tr_vals, tr_cols, rf_vals, rf_cols):
@@ -419,11 +413,11 @@
             dma((2 * row_blocks,)),
             dma((tasks,)),
             dma((tasks, RING - 1)),
+            dma((2,)),
+            dma((tasks, 2)),
+            dma,
             dma((tasks,)),
-            dma((tasks, 2)),
-            dma((tasks,)),
-            dma((tasks,)),
-            dma((tasks,)),
+            dma,
         ],
         compiler_params=pltpu.CompilerParams(
             collective_id=0,

time: 194 us -> 193 us (level)
  no operation moved by 1% of the time
where the time goes in v6:
time: 193 us
  Pallas kernels  191 us (99%)
    pallas_call x1, Pallas kernels, shards(): pl.pallas_call(functools.partial(kernel, (batches, width, blocks, row_blo...  191 us

profile of v6, /device:TPU:1, one launch (start us, length us, event | category | flops | bytes accessed | tf_op | source)
XLA Modules:
  0.0 192.8 jit_solution(9876754199192716325)
XLA Ops:
  0.0 191.0 %shard_map.55 = f32[384,256]{1,0:T(8,128)} custom-call(f32[384,256]{1,0:T(8,128)} %bitcast.9, f32[6,12,128,128]{3,2,1,0:T(8,128)} %bitcast.6, f32[6,12,128,128]{3,2,1,0:T(8,128)} %bitcast.7, s32[6,1,12]{2,1,0:T(1,128)} %bitcast.10, s32[6,1,12]{2,1,0:T(1,128)} %bitcast.11), custom_call_target="tpu_custom_call" | custom-call | tf_op jit(solution)/shard_map/pallas_call | solution.py:393
  191.1 1.8 copy.7
